TPU v7x, 128 devices: a whole 4x4x4 slice. The times are simulated.
128 devices in a mesh: group: 8 (over x_lo, z), tensor: 16 (over x_hi, y, core).
Axes of the slice: x: 4 (x_hi: 2, x_lo: 2; x = x_hi * 2 + x_lo), y: 4, z: 4, core: 2. Of those that a mesh axis runs over, the one named last changes fastest.
Arguments:
- hidden: bfloat16 [12288, 2048], P(('group', 'tensor')), may hold values from -20 to 20
- request_of: int32 [12288], P('group'), may hold values from 0 to 191, as said below
- positions: int32 [12288], P('group'), may hold values from 0 to 511, as said below
- page_table: int32 [8, 64], P('group'), may hold values from 0 to 63, each once within a row
- attn_gain: float32 [2048], replicated, may hold values from 0.5 to 1.5
- mlp_gain: float32 [2048], replicated, may hold values from 0.5 to 1.5
- wq: float32 [2048, 2048], P('group', 'tensor'), may hold values from -2 to 2
- wk: float32 [2048, 1024], P('group', 'tensor'), may hold values from -1 to 1
- wv: float32 [2048, 1024], P('group', 'tensor'), may hold values from -0.125 to 0.125
- wo: float32 [2048, 2048], P('tensor', 'group'), may hold values from -0.125 to 0.125
- w_gate: float32 [2048, 8192], P('group', 'tensor'), may hold values from -0.125 to 0.125
- w_up: float32 [2048, 8192], P('group', 'tensor'), may hold values from -0.125 to 0.125
- w_down: float32 [8192, 2048], P('tensor', 'group'), may hold values from -0.0625 to 0.0625
Outputs:
- layer_out: bfloat16 [12288, 2048], P(('group', 'tensor'))
- kv_pages: bfloat16 [512, 128, 2048], P('group', None, 'tensor')
Inputs may be any that keep to these rules, and one draw needn't show every extreme that they name: `request_of`: prompt numbers rise strictly along the token stream, starting at 0, and the last prompt of the stream has the number 12288 // 64 - 1; a prompt's rows are consecutive, and a prompt that reaches the last row of one block of 1536 rows continues at the first row of the next block. A prompt's rows have positions 0, 1, 2 and so on in order; a prompt has at most 512 rows, and one has exactly 512.
All inputs are finite; a program needn't handle non-finite values.
Results may differ from a plain program's by a relative error of at most 0.014.
Values may be sent and summed in bfloat16 or wider, within the bound.
A program may use at most 128 MiB of HBM per device.

v0:
```python
import jax
import jax.numpy as jnp
from jax import lax
from jax.sharding import PartitionSpec as P

QH = 16
KVH = 8
HD = 128
PAGE = 128


rope_base = 1000000.0
norm_eps = 1e-06


def partner(value, axis, distance):
    mask = 2**distance
    pairs = [(source, source ^ mask) for source in range(lax.axis_size(axis))]
    return lax.ppermute(value, axis, pairs)


def from_behind(block, axis, distance):
    devices = range(lax.axis_size(axis))
    route = [(i - distance, i) for i in devices if i - distance in devices]
    return lax.ppermute(block, axis, route)


def rms_scale(values, gain):
    square = jnp.mean(values * values, axis=-1, keepdims=True)
    return (values * lax.rsqrt(square + norm_eps) * gain).astype(jnp.bfloat16)


def rotate(values, places):
    half_dim = values.shape[-1] // 2
    frequency = rope_base ** (-(jnp.arange(half_dim, dtype=jnp.float32) * 2.0 / values.shape[-1]))
    angle = places.astype(jnp.float32)[:, None] * frequency[None, :]
    cosine = jnp.cos(angle)[:, None, :]
    sine = jnp.sin(angle)[:, None, :]
    widened = values.astype(jnp.float32)
    first = widened[..., :half_dim]
    second = widened[..., half_dim:]
    return jnp.concatenate(
        [first * cosine - second * sine, second * cosine + first * sine], axis=-1
    ).astype(jnp.bfloat16)


def join_halves(own_part, other_part):
    even = lax.axis_index("tensor") % 2 == 0
    lower = jnp.where(even, own_part, other_part)
    upper = jnp.where(even, other_part, own_part)
    return jnp.concatenate([lower, upper], axis=-1)


def contract_rows(acts, pieces):
    return tuple((jnp.dot(acts, piece, preferred_element_type=jnp.float32) for piece in pieces))


def body(
    hidden,
    request_of,
    positions,
    page_table,
    attn_gain,
    mlp_gain,
    wq,
    wk,
    wv,
    wo,
    w_gate,
    w_up,
    w_down,
):
    tensor_count = lax.axis_size("tensor")
    rows_dev = hidden.shape[0]
    tok_group = request_of.shape[0]
    query_heads = QH // tensor_count
    key_heads = max(1, KVH // tensor_count)
    group_ratio = QH // KVH
    residual = lax.all_gather(hidden, "tensor", axis=0, tiled=True).astype(jnp.float32)
    normed = rms_scale(residual, attn_gain)
    query_rows = wq.astype(jnp.bfloat16)
    key_rows = wk.astype(jnp.bfloat16)
    value_rows = wv.astype(jnp.bfloat16)
    other_key, other_value = partner((key_rows, value_rows), "tensor", 0)
    key_rows = join_halves(key_rows, other_key)
    value_rows = join_halves(value_rows, other_value)
    query_sum, key_sum, value_sum = contract_rows(
        normed,
        (
            lax.all_gather(query_rows, "group", axis=0, tiled=True),
            lax.all_gather(key_rows, "group", axis=0, tiled=True),
            lax.all_gather(value_rows, "group", axis=0, tiled=True),
        ),
    )
    query_raw = query_sum.astype(jnp.bfloat16)
    key_raw = key_sum.astype(jnp.bfloat16)
    value_raw = value_sum.astype(jnp.bfloat16)
    queries = rotate(query_raw.reshape(tok_group, query_heads, HD), positions)
    keys = rotate(key_raw.reshape(tok_group, key_heads, HD), positions)
    values = value_raw.reshape(tok_group, key_heads, HD)
    kv_rows = jnp.stack([keys, values], axis=2)
    earlier = from_behind(kv_rows, "group", 1)
    earlier_rows = earlier.shape[0]
    all_rows = jnp.concatenate([earlier, kv_rows], axis=0)
    all_keys = jnp.repeat(all_rows[:, :, 0], group_ratio, axis=1)[:, :query_heads]
    all_values = jnp.repeat(all_rows[:, :, 1], group_ratio, axis=1)[:, :query_heads]
    first_request = request_of[0]
    first_position = positions[0]
    same_local = (request_of[:, None] == request_of[None, :]) & (
        positions[None, :] <= positions[:, None]
    )
    same_earlier = (request_of[:, None] == first_request) & (
        jnp.arange(earlier_rows)[None, :] >= earlier_rows - first_position
    )
    visible = jnp.concatenate([same_earlier, same_local], axis=1)
    scores = jnp.einsum(
        "qhd,khd->hqk", queries, all_keys, preferred_element_type=jnp.float32
    ) * HD ** (-0.5)
    scores = jnp.where(visible[None], scores, -1e30)
    row_peak = jnp.max(scores, axis=-1, keepdims=True)
    probs = jnp.where(visible[None], jnp.exp(scores - row_peak), 0.0)
    total = jnp.sum(probs, axis=-1, keepdims=True)
    mixed_heads = jnp.einsum(
        "hqk,khd->qhd", probs.astype(jnp.bfloat16), all_values, preferred_element_type=jnp.float32
    ) / jnp.transpose(total, (1, 0, 2))
    attended = mixed_heads.astype(jnp.bfloat16).reshape(tok_group, query_heads * HD)
    out_rows = wo.astype(jnp.bfloat16)
    attn_part = jnp.dot(
        attended,
        lax.all_gather(out_rows, "group", axis=1, tiled=True),
        preferred_element_type=jnp.float32,
    )
    mixed = residual + lax.psum(attn_part.astype(jnp.bfloat16), "tensor").astype(jnp.float32)
    normed_mlp = rms_scale(mixed, mlp_gain)
    gate_rows = w_gate.astype(jnp.bfloat16)
    up_rows = w_up.astype(jnp.bfloat16)
    gate_sum, up_sum = contract_rows(
        normed_mlp,
        (
            lax.all_gather(gate_rows, "group", axis=0, tiled=True),
            lax.all_gather(up_rows, "group", axis=0, tiled=True),
        ),
    )
    activation = (jax.nn.silu(gate_sum) * up_sum).astype(jnp.bfloat16)
    down_rows = w_down.astype(jnp.bfloat16)
    down_part = jnp.dot(
        activation,
        lax.all_gather(down_rows, "group", axis=1, tiled=True),
        preferred_element_type=jnp.float32,
    )
    summed = lax.psum(down_part.astype(jnp.bfloat16), "tensor").astype(jnp.float32)
    first_row = lax.axis_index("tensor") * rows_dev
    own_mixed = lax.dynamic_slice_in_dim(mixed, first_row, rows_dev, 0)
    own_summed = lax.dynamic_slice_in_dim(summed, first_row, rows_dev, 0)
    layer_out = (own_mixed + own_summed).astype(jnp.bfloat16)
    pages = page_table.shape[1]
    changed = jnp.concatenate(
        [jnp.ones((1,), jnp.int32), (request_of[1:] != request_of[:-1]).astype(jnp.int32)]
    )
    opens = jnp.maximum(changed, (positions % PAGE == 0).astype(jnp.int32))
    logical = jnp.cumsum(opens) - 1
    chosen = jnp.sum(
        jnp.where(logical[:, None] == jnp.arange(pages)[None, :], page_table, 0), axis=1
    )
    target = chosen * PAGE + positions % PAGE
    width = 2 * KVH * HD // tensor_count
    flat_rows = kv_rows.reshape(tok_group, key_heads * 2 * HD)
    offset = lax.axis_index("tensor") * width % (key_heads * 2 * HD)
    own_slice = lax.dynamic_slice_in_dim(flat_rows, offset, width, 1)
    cache = jnp.zeros((pages * PAGE, width), jnp.bfloat16).at[target].set(own_slice)
    return (layer_out, cache.reshape(pages, PAGE, width))


def solution(mesh):
    placed = (
        P(("group", "tensor"), None),
        P("group"),
        P("group"),
        P("group", None),
        P(),
        P(),
        P("group", "tensor"),
        P("group", "tensor"),
        P("group", "tensor"),
        P("tensor", "group"),
        P("group", "tensor"),
        P("group", "tensor"),
        P("tensor", "group"),
    )
    return jax.shard_map(
        body,
        mesh=mesh,
        in_specs=placed,
        out_specs=(P(("group", "tensor"), None), P("group", None, "tensor")),
        check_vma=False,
    )
```

profile of v0, /device:TPU:2, one launch (start us, length us, event | category | flops | bytes accessed | tf_op | source)
XLA Modules:
  0.0 592.4 jit_solution(9900236413319749413)
XLA Ops:
  11.0 0.9 convert_element_type.110
  11.9 1.2 slice.43
  13.1 1.2 slice.42
  14.3 0.8 slice_compare_fusion
  16.3 0.9 convert_element_type.117
  18.9 1.4 iota_compare_fusion.1
  21.0 29.8 %all_gather.27 = bf16[2048,128]{1,0:T(8,128)(2,1)S(1)} all-gather(bf16[256,128]{1,0:T(8,128)(2,1)S(1)} %convert_element_type.110), channel_id=1, replica_groups=mesh['group'=8,'tensor'=16] {'group'}, dimensions={0}, use_global_device_ids=true | all-gather | bytes 589824 | tf_op jit(solution)/shard_map/all_gather | solution.py:90
  50.8 32.2 %all_gather.28 = bf16[128,2048]{1,0:T(8,128)(2,1)} all-gather(bf16[128,256]{1,0:T(8,128)(2,1)S(1)} %convert_element_type.117), channel_id=1, replica_groups=mesh['group'=8,'tensor'=16] {'group'}, dimensions={1}, use_global_device_ids=true | all-gather | bytes 589824 | tf_op jit(solution)/shard_map/all_gather | solution.py:130
  83.0 3.3 compare_and_fusion
  86.5 29.2 %all_gather.25 = bf16[2048,128]{0,1:T(8,128)(2,1)S(1)} all-gather(bf16[256,128]{0,1:T(8,128)(2,1)S(1)} %pad_maximum_fusion.1), channel_id=1, replica_groups=mesh['group'=8,'tensor'=16] {'group'}, dimensions={0}, use_global_device_ids=true | all-gather | bytes 589824 | tf_op jit(solution)/shard_map/all_gather | solution.py:91
  115.7 30.8 %all_gather.26 = bf16[2048,128]{0,1:T(8,128)(2,1)} all-gather(bf16[256,128]{0,1:T(8,128)(2,1)S(1)} %pad_maximum_fusion.2), channel_id=1, replica_groups=mesh['group'=8,'tensor'=16] {'group'}, dimensions={0}, use_global_device_ids=true | all-gather | bytes 589824 | tf_op jit(solution)/shard_map/all_gather | solution.py:92
  146.5 4.2 fusion.1
  151.1 1.5 fusion.3
  152.6 2.2 fusion.13
  154.8 2.2 fusion.16
  157.1 2.2 fusion.14
  159.3 1.7 fusion.52
  161.1 4.3 collective-permute-start.2
  165.4 1.5 broadcast_and_fusion
  167.0 10.1 %collective-permute-done.2 = bf16[1536,1,2,128]{0,3,2,1:T(8,128)(2,1)S(1)} collective-permute-done((bf16[1536,1,2,128]{0,3,2,1:T(8,128)(2,1)S(1)}, bf16[1536,1,2,128]{0,3,2,1:T(8,128)(2,1)S(1)}, u32[]{:S(2)}, u32[]{:S(2)}) %collective-permute-start.2) | collective-permute-done | bytes 786464 | tf_op jit(solution)/shard_map/ppermute | solution.py:25
  177.3 4.1 fusion
  181.4 6.4 %copy-done.1 = f32[1536,3072]{1,0:T(8,128)} copy-done((f32[1536,3072]{1,0:T(8,128)}, f32[1536,3072]{1,0:T(8,128)S(1)}, u32[]{:S(2)}) %copy-start.1) | copy-done | bytes 18874392
  187.8 6.4 %fusion.4 = f32[1536]{0:T(1024)S(1)} fusion(f32[1536,3072]{1,0:T(8,128)S(1)} %get-tuple-element.17, f32[1536]{0:T(1024)S(1)} %get-tuple-element.16, pred[1536,1536]{1,0:T(32,128)(4,1)S(1)} %compare_and_fusion, pred[1536,1536]{1,0:T(32,128)(4,1)S(1)} %broadcast_and_fusion), kind=kLoop, calls=%fused_computation.13 | loop fusion | flops 28310016 | bytes 23605248 | tf_op jit(solution)/shard_map/reduce_sum | solution.py:122
  194.2 14.1 %convolution_convert_fusion.1 = bf16[1536,2048]{1,0:T(8,128)(2,1)} fusion(bf16[128,2048]{1,0:T(8,128)(2,1)} %all_gather.28, f32[1536,3072]{1,0:T(8,128)} %copy-done.1, f32[1536]{0:T(1024)S(1)} %get-tuple-element.16, bf16[3072,1,2,128]{0,3,2,1:T(8,128)(2,1)} %copy-done.3, f32[1536]{0:T(1024)S(1)} %fusion.4, pred[1536,1536]{1,0:T(32,128)(4,1)S(1)} %compare_and_fusion, ...), kind=kOutput, calls=%fused_computation.18 | convolution fusion | flops 2045116416 | bytes 31207424 | tf_op jit(solution)/shard_map/dot_general | solution.py:128
  208.4 1.0 copy-done.4
  212.1 176.7 %all-reduce.3.cloned.1.call-done = bf16[1536,2048]{1,0:T(8,128)(2,1)} async-done(((bf16[1536,2048]{1,0:T(8,128)(2,1)}), bf16[1536,2048]{1,0:T(8,128)(2,1)}) %all-reduce.3.cloned.1.call-update) | async-done | bytes 6291472 | tf_op jit(solution)/shard_map/psum | solution.py:133
  388.7 11.2 %multiply_reduce_fusion = (f32[1536]{0:T(1024)S(1)}, f32[1536,2048]{1,0:T(8,128)}) fusion(bf16[1536,2048]{1,0:T(8,128)(2,1)} %all-reduce.3.cloned.1.call-done, bf16[1536,2048]{1,0:T(8,128)(2,1)} %all-gather.5.cloned.1.call-done), kind=kLoop, calls=%fused_computation.12 | loop fusion | flops 15727104 | bytes 25171968 | tf_op jit(solution)/shard_map/reduce_sum | solution.py:29
  400.0 10.4 %fusion.64 = f32[1536,512]{1,0:T(8,128)} fusion(bf16[2048,512]{1,0:T(8,128)(2,1)} %all-gather.7.cloned.1.call-done, f32[2048]{0:T(1024)S(1)} %copy-done.11, f32[1536]{0:T(1024)S(1)} %add_rsqrt_fusion, bf16[1536,2048]{1,0:T(8,128)(2,1)} %all-gather.5.cloned.1.call-done, bf16[1536,2048]{1,0:T(8,128)(2,1)} %all-reduce.3.cloned.1.call-done), kind=kOutput, calls=%fused_computation.96 | convolution fusion | flops 3240099840 | bytes 17840128 | tf_op jit(solution)/shard_map/dot_general | solution.py:55
  410.4 15.3 %convolution_convert_fusion = bf16[1536,2048]{1,0:T(8,128)(2,1)} fusion(bf16[512,2048]{1,0:T(8,128)(2,1)} %all-gather.11.cloned.1.call-done, bf16[2048,512]{1,0:T(8,128)(2,1)} %all-gather.9.cloned.1.call-done, f32[1536,512]{1,0:T(8,128)} %fusion.64, f32[2048]{0:T(1024)S(1)} %copy-done.11, f32[1536]{0:T(1024)S(1)} %add_rsqrt_fusion, ...), kind=kOutput, calls=%fused_computation.17 | convolution fusion | flops 6469189632 | bytes 26228736 | tf_op jit(solution)/shard_map/dot_general | solution.py:146
  426.0 6.1 %scatter_custom_fusion = bf16[8192,128]{1,0:T(8,128)(2,1)} fusion(s32[1536]{0:T(1024)S(1)} %get-tuple-element.14, bf16[1536,128]{1,0:T(8,128)(2,1)S(1)} %copy.17, bf16[]{:T(256)} %constant.84.clone.1), kind=kCustom, calls=%fused_computation.35 | custom fusion | bytes 2097154 | tf_op jit(solution)/shard_map/scatter | solution.py:170
  432.1 150.9 %all-reduce.5.cloned.1.call-done = bf16[1536,2048]{1,0:T(8,128)(2,1)} async-done(((bf16[1536,2048]{1,0:T(8,128)(2,1)}), bf16[1536,2048]{1,0:T(8,128)(2,1)}) %all-reduce.5.cloned.1.call-update) | async-done | bytes 6291472 | tf_op jit(solution)/shard_map/psum | solution.py:151
  583.0 2.1 add_convert_fusion
  (65 shorter events, 9.5 us)
Async XLA Ops:
  8.0 78.4 %copy-start.9 = (f32[256,64]{0,1:T(8,128)S(1)}, f32[256,64]{0,1:T(8,128)}, u32[]{:S(2)}) copy-start(f32[256,64]{0,1:T(8,128)} %param.20) | copy-start | bytes 196612
  8.0 78.4 %copy-start.8 = (f32[256,64]{0,1:T(8,128)S(1)}, f32[256,64]{0,1:T(8,128)}, u32[]{:S(2)}) copy-start(f32[256,64]{0,1:T(8,128)} %param.21) | copy-start | bytes 196612
  8.0 138.5 %all-gather.5.cloned.1.call-start = ((), (), s32[]{:S(2)}) async-start(), calls=%async_computation | async-start | bytes 6684672 | tf_op jit(solution)/shard_map/all_gather | solution.py:79
  8.8 380.0 %all-reduce.3.cloned.1.call-start = ((), (), s32[]{:S(2)}) async-start(), calls=%async_computation.1 | async-start | bytes 12582912 | tf_op jit(solution)/shard_map/psum | solution.py:133
  9.6 76.7 %collective-permute-start = (bf16[256,64]{0,1:T(8,128)(2,1)S(1)}, bf16[256,64]{0,1:T(8,128)(2,1)S(1)}, u32[]{:S(2)}, u32[]{:S(2)}) collective-permute-start(bf16[256,64]{0,1:T(8,128)(2,1)S(1)} %convert_element_type.103), channel_id=1, source_target_pairs={{0,1},{1,0},{2,3},{3,2},{4,5},{5,4},{6,7},{7,6},{8,9},{9,8},{10,11... | collective-permute-start | bytes 98312 | tf_op jit(solution)/shard_map/ppermute | solution.py:19
  10.5 75.9 %collective-permute-start.1 = (bf16[256,64]{0,1:T(8,128)(2,1)S(1)}, bf16[256,64]{0,1:T(8,128)(2,1)S(1)}, u32[]{:S(2)}, u32[]{:S(2)}) collective-permute-start(bf16[256,64]{0,1:T(8,128)(2,1)S(1)} %convert_element_type.108), channel_id=1, source_target_pairs={{0,1},{1,0},{2,3},{3,2},{4,5},{5,4},{6,7},{7,6},{8,9},{9,8},{10,11... | collective-permute-start | bytes 98312 | tf_op jit(solution)/shard_map/ppermute | solution.py:19
  83.0 67.7 %copy-start.10 = (f32[2048]{0:T(1024)S(1)}, f32[2048]{0:T(1024)}, u32[]{:S(2)}) copy-start(f32[2048]{0:T(1024)} %param.17) | copy-start | bytes 24580
  146.5 4.6 copy-start
  154.8 2.2 copy-start.7
  161.1 16.0 %collective-permute-start.2 = (bf16[1536,1,2,128]{0,3,2,1:T(8,128)(2,1)S(1)}, bf16[1536,1,2,128]{0,3,2,1:T(8,128)(2,1)S(1)}, u32[]{:S(2)}, u32[]{:S(2)}) collective-permute-start(bf16[1536,1,2,128]{0,3,2,1:T(8,128)(2,1)S(1)} %pad_maximum_fusion), channel_id=1, source_target_pairs={{0,16},{16,32},{32,48},{48,64},{64,80},{80,96},{96,112},{1,17},{17... | collective-permute-start | bytes 2359304 | tf_op jit(solution)/shard_map/ppermute | solution.py:25
  167.0 14.4 %copy-start.2 = (pred[1536,1536]{1,0:T(32,128)(4,1)}, pred[1536,1536]{1,0:T(32,128)(4,1)S(1)}, u32[]{:S(2)}) copy-start(pred[1536,1536]{1,0:T(32,128)(4,1)S(1)} %broadcast_and_fusion) | copy-start | bytes 7077892
  177.3 4.1 copy-start.3
  181.4 6.5 %copy-start.1 = (f32[1536,3072]{1,0:T(8,128)}, f32[1536,3072]{1,0:T(8,128)S(1)}, u32[]{:S(2)}) copy-start(f32[1536,3072]{1,0:T(8,128)S(1)} %get-tuple-element.17) | copy-start | bytes 56623108
  208.3 1.0 copy-start.4
  208.3 1.9 copy-start.5
  208.3 2.7 copy-start.6
  208.4 191.6 %all-gather.7.cloned.1.call-start = ((), (), s32[]{:S(2)}) async-start(), calls=%async_computation.2 | async-start | bytes 2359296 | tf_op jit(solution)/shard_map/all_gather | solution.py:140
  210.2 200.2 %all-gather.11.cloned.1.call-start = ((), (), s32[]{:S(2)}) async-start(), calls=%async_computation.4 | async-start | bytes 2359296 | tf_op jit(solution)/shard_map/all_gather | solution.py:148
  211.0 199.4 %all-gather.9.cloned.1.call-start = ((), (), s32[]{:S(2)}) async-start(), calls=%async_computation.3 | async-start | bytes 2359296 | tf_op jit(solution)/shard_map/all_gather | solution.py:141
  211.8 188.1 %copy-start.11 = (f32[2048]{0:T(1024)S(1)}, f32[2048]{0:T(1024)}, u32[]{:S(2)}) copy-start(f32[2048]{0:T(1024)} %param.18) | copy-start | bytes 24580
  211.8 371.2 %all-reduce.5.cloned.1.call-start = ((), (), s32[]{:S(2)}) async-start(), calls=%async_computation.5 | async-start | bytes 12582912 | tf_op jit(solution)/shard_map/psum | solution.py:151
Sparse Core Ops, SparseCore 0:
  11.3 69.3 all-gather.4
  208.5 180.2 all-reduce.2
  425.8 157.1 all-reduce.4
Sparse Core Ops, SparseCore 1:
  210.5 47.0 all-gather.6
  259.6 44.7 all-gather.10
  306.4 46.4 all-gather.8
where the time goes:
time: 594 us; the launch traced here: 592 us
  waiting for transfers between devices  338 us (57%)
  blocking collectives  122 us (21%)
  matrix products  50.5 us (9%)
  other arithmetic  42.9 us (7%)
  local copies, waits for them, and re-layouts  16.7 us (3%)
  between operations  16.4 us (3%)
    psum x1, waiting for transfers between devices, body(): lax.psum(attn_part.astype(jnp.bfloat16), 'tensor').astype(jnp.float32)  177 us
    psum x1, waiting for transfers between devices, body(): lax.psum(down_part.astype(jnp.bfloat16), 'tensor').astype(jnp.float32)  151 us
    all_gather x1, blocking collectives, body(): lax.all_gather(out_rows, 'group', axis=1, tiled=True)  32.2 us
    all_gather x1, blocking collectives, body(): lax.all_gather(value_rows, 'group', axis=0, tiled=True)  30.8 us
    all_gather x1, blocking collectives, body(): lax.all_gather(query_rows, 'group', axis=0, tiled=True)  29.8 us
    all_gather x1, blocking collectives, body(): lax.all_gather(key_rows, 'group', axis=0, tiled=True)  29.2 us
    dot_general x4, matrix products, contract_rows(): jnp.dot(acts, piece, preferred_element_type=jnp.float32)  17 us
    reduce_sum x2, other arithmetic, rms_scale(): square = jnp.mean(values * values, axis=-1, keepdims=True)  15.4 us
  transfers between devices with their start and end apart: 9, of which 3 were waited for; matrix products, arithmetic and copies ran while one was open for 8% of the time, Pallas kernels for 0%

commit v1 on v0

--- a/solution.py
+++ b/solution.py
@@ -7,6 +7,7 @@
 KVH = 8
 HD = 128
 PAGE = 128
+MAXLEN = 512
 
 
 rope_base = 1000000.0
@@ -51,8 +52,10 @@
     return jnp.concatenate([lower, upper], axis=-1)
 
 
-def contract_rows(acts, pieces):
-    return tuple((jnp.dot(acts, piece, preferred_element_type=jnp.float32) for piece in pieces))
+def dot_t(acts, weight_t):
+    return lax.dot_general(
+        acts, weight_t, (((1,), (1,)), ((), ())), preferred_element_type=jnp.float32
+    )
 
 
 def body(
@@ -71,36 +74,41 @@
     w_down,
 ):
     tensor_count = lax.axis_size("tensor")
-    rows_dev = hidden.shape[0]
     tok_group = request_of.shape[0]
     query_heads = QH // tensor_count
     key_heads = max(1, KVH // tensor_count)
     group_ratio = QH // KVH
-    residual = lax.all_gather(hidden, "tensor", axis=0, tiled=True).astype(jnp.float32)
-    normed = rms_scale(residual, attn_gain)
-    query_rows = wq.astype(jnp.bfloat16)
-    key_rows = wk.astype(jnp.bfloat16)
-    value_rows = wv.astype(jnp.bfloat16)
+    bf = jnp.bfloat16
+    residual = hidden.astype(jnp.float32)
+    normed = lax.all_gather(rms_scale(residual, attn_gain), "tensor", axis=0, tiled=True)
+    key_rows = wk.astype(bf)
+    value_rows = wv.astype(bf)
     other_key, other_value = partner((key_rows, value_rows), "tensor", 0)
     key_rows = join_halves(key_rows, other_key)
     value_rows = join_halves(value_rows, other_value)
-    query_sum, key_sum, value_sum = contract_rows(
-        normed,
-        (
-            lax.all_gather(query_rows, "group", axis=0, tiled=True),
-            lax.all_gather(key_rows, "group", axis=0, tiled=True),
-            lax.all_gather(value_rows, "group", axis=0, tiled=True),
-        ),
-    )
-    query_raw = query_sum.astype(jnp.bfloat16)
-    key_raw = key_sum.astype(jnp.bfloat16)
-    value_raw = value_sum.astype(jnp.bfloat16)
+    q_cols = query_heads * HD
+    kv_cols = key_heads * HD
+    attn_w = jnp.concatenate([wq.astype(bf), key_rows, value_rows, wo.astype(bf).T], axis=1)
+    attn_w = lax.all_gather(attn_w, "group", axis=0, tiled=True)
+    query_w = attn_w[:, :q_cols]
+    key_w = attn_w[:, q_cols : q_cols + kv_cols]
+    value_w = attn_w[:, q_cols + kv_cols : q_cols + 2 * kv_cols]
+    out_w_t = attn_w[:, q_cols + 2 * kv_cols :]
+    ff_cols = w_gate.shape[1]
+    mlp_w = jnp.concatenate([w_gate.astype(bf), w_up.astype(bf), w_down.astype(bf).T], axis=1)
+    mlp_w = lax.all_gather(mlp_w, "group", axis=0, tiled=True)
+    gate_w = mlp_w[:, :ff_cols]
+    up_w = mlp_w[:, ff_cols : 2 * ff_cols]
+    down_w_t = mlp_w[:, 2 * ff_cols :]
+    query_raw = jnp.dot(normed, query_w, preferred_element_type=jnp.float32).astype(bf)
+    key_raw = jnp.dot(normed, key_w, preferred_element_type=jnp.float32).astype(bf)
+    value_raw = jnp.dot(normed, value_w, preferred_element_type=jnp.float32).astype(bf)
     queries = rotate(query_raw.reshape(tok_group, query_heads, HD), positions)
     keys = rotate(key_raw.reshape(tok_group, key_heads, HD), positions)
     values = value_raw.reshape(tok_group, key_heads, HD)
     kv_rows = jnp.stack([keys, values], axis=2)
-    earlier = from_behind(kv_rows, "group", 1)
-    earlier_rows = earlier.shape[0]
+    earlier_rows = min(MAXLEN, tok_group)
+    earlier = from_behind(kv_rows[tok_group - earlier_rows :], "group", 1)
     all_rows = jnp.concatenate([earlier, kv_rows], axis=0)
     all_keys = jnp.repeat(all_rows[:, :, 0], group_ratio, axis=1)[:, :query_heads]
     all_values = jnp.repeat(all_rows[:, :, 1], group_ratio, axis=1)[:, :query_heads]
@@ -121,38 +129,19 @@
     probs = jnp.where(visible[None], jnp.exp(scores - row_peak), 0.0)
     total = jnp.sum(probs, axis=-1, keepdims=True)
     mixed_heads = jnp.einsum(
-        "hqk,khd->qhd", probs.astype(jnp.bfloat16), all_values, preferred_element_type=jnp.float32
+        "hqk,khd->qhd", probs.astype(bf), all_values, preferred_element_type=jnp.float32
     ) / jnp.transpose(total, (1, 0, 2))
-    attended = mixed_heads.astype(jnp.bfloat16).reshape(tok_group, query_heads * HD)
-    out_rows = wo.astype(jnp.bfloat16)
-    attn_part = jnp.dot(
-        attended,
-        lax.all_gather(out_rows, "group", axis=1, tiled=True),
-        preferred_element_type=jnp.float32,
-    )
-    mixed = residual + lax.psum(attn_part.astype(jnp.bfloat16), "tensor").astype(jnp.float32)
-    normed_mlp = rms_scale(mixed, mlp_gain)
-    gate_rows = w_gate.astype(jnp.bfloat16)
-    up_rows = w_up.astype(jnp.bfloat16)
-    gate_sum, up_sum = contract_rows(
-        normed_mlp,
-        (
-            lax.all_gather(gate_rows, "group", axis=0, tiled=True),
-            lax.all_gather(up_rows, "group", axis=0, tiled=True),
-        ),
-    )
-    activation = (jax.nn.silu(gate_sum) * up_sum).astype(jnp.bfloat16)
-    down_rows = w_down.astype(jnp.bfloat16)
-    down_part = jnp.dot(
-        activation,
-        lax.all_gather(down_rows, "group", axis=1, tiled=True),
-        preferred_element_type=jnp.float32,
-    )
-    summed = lax.psum(down_part.astype(jnp.bfloat16), "tensor").astype(jnp.float32)
-    first_row = lax.axis_index("tensor") * rows_dev
-    own_mixed = lax.dynamic_slice_in_dim(mixed, first_row, rows_dev, 0)
-    own_summed = lax.dynamic_slice_in_dim(summed, first_row, rows_dev, 0)
-    layer_out = (own_mixed + own_summed).astype(jnp.bfloat16)
+    attended = mixed_heads.astype(bf).reshape(tok_group, query_heads * HD)
+    attn_part = dot_t(attended, out_w_t)
+    attn_sum = lax.psum_scatter(attn_part.astype(bf), "tensor", scatter_dimension=0, tiled=True)
+    mixed = residual + attn_sum.astype(jnp.float32)
+    normed_mlp = lax.all_gather(rms_scale(mixed, mlp_gain), "tensor", axis=0, tiled=True)
+    gate_sum = jnp.dot(normed_mlp, gate_w, preferred_element_type=jnp.float32)
+    up_sum = jnp.dot(normed_mlp, up_w, preferred_element_type=jnp.float32)
+    activation = (jax.nn.silu(gate_sum) * up_sum).astype(bf)
+    down_part = dot_t(activation, down_w_t)
+    summed = lax.psum_scatter(down_part.astype(bf), "tensor", scatter_dimension=0, tiled=True)
+    layer_out = (mixed + summed.astype(jnp.float32)).astype(bf)
     pages = page_table.shape[1]
     changed = jnp.concatenate(
         [jnp.ones((1,), jnp.int32), (request_of[1:] != request_of[:-1]).astype(jnp.int32)]

time: 594 us -> 533 us (0.90)
  blocking collectives: 122 us -> 0 us
  waiting for transfers between devices: 338 us -> 420 us
  other arithmetic: 42.9 us -> 26.3 us
    psum x2 -> x0, waiting for transfers between devices: 328 us -> none  [the longest x1 177 us: body(): lax.psum(attn_part.astype(jnp.bfloat16), 'tensor').astype(jnp.float32)]
    all_gather x4, waiting for transfers between devices: 0.01 us -> 249 us  [the longest x1 76.9 us: body(): mlp_w = lax.all_gather(mlp_w, 'group', axis=0, tiled=True)]
    reduce_scatter x0 -> x2, waiting for transfers between devices: none -> 163 us  [the longest x1 83.1 us: body(): lax.psum_scatter(attn_part.astype(bf), 'tensor', scatter_dimension=0, til...]
    all_gather x4 -> x0, blocking collectives: 122 us -> none  [the longest x1 32.2 us: body(): lax.all_gather(out_rows, 'group', axis=1, tiled=True)]
    reduce_sum x2, other arithmetic: 15.4 us -> 2.39 us  [rms_scale(): square = jnp.mean(values * values, axis=-1, keepdims=True)]
  transfers between devices with their start and end apart: 9 -> 9, of which waited for: 3 -> 7; matrix products, arithmetic and copies ran while one was open for 8% -> 5% of each run, Pallas kernels for 0% -> 0%
where the time goes in v1:
time: 533 us; the launch traced here: 531 us
  waiting for transfers between devices  420 us (79%)
  matrix products  46.5 us (9%)
  other arithmetic  26.3 us (5%)
  local copies, waits for them, and re-layouts  18.4 us (3%)
  between operations  15.1 us (3%)
    reduce_scatter x1, waiting for transfers between devices, body(): lax.psum_scatter(attn_part.astype(bf), 'tensor', scatter_dimension=0, til...  83.1 us
    reduce_scatter x1, waiting for transfers between devices, body(): lax.psum_scatter(down_part.astype(bf), 'tensor', scatter_dimension=0, til...  80.1 us
    all_gather x1, waiting for transfers between devices, body(): mlp_w = lax.all_gather(mlp_w, 'group', axis=0, tiled=True)  76.9 us
    all_gather x1, waiting for transfers between devices, body(): lax.all_gather(rms_scale(residual, attn_gain), 'tensor', axis=0, tiled=True)  67.7 us
    all_gather x1, waiting for transfers between devices, body(): lax.all_gather(rms_scale(mixed, mlp_gain), 'tensor', axis=0, tiled=True)  67.5 us
    all_gather x1, waiting for transfers between devices, body(): attn_w = lax.all_gather(attn_w, 'group', axis=0, tiled=True)  36.6 us
    dot_general x2, matrix products, dot_t(): lax.dot_general(acts, weight_t, (((1,), (1,)), ((), ())), preferred_eleme...  23.2 us
  transfers between devices with their start and end apart: 9, of which 7 were waited for; matrix products, arithmetic and copies ran while one was open for 5% of the time, Pallas kernels for 0%

profile of v1, /device:TPU:2, one launch (start us, length us, event | category | flops | bytes accessed | tf_op | source)
XLA Modules:
  0.0 531.3 jit_solution(18417483994297506273)
XLA Ops:
  9.4 1.0 copy.22
  13.9 0.9 bitcast_dynamic-update-slice_fusion
  15.6 1.2 fusion.33
  16.8 1.9 fusion.35
  18.8 1.2 slice.69
  19.9 1.2 slice.70
  24.0 2.4 compare_and_fusion
  26.5 36.6 %all-gather.7.cloned.1.call-done = bf16[2048,512]{0,1:T(8,128)(2,1)} async-done(((bf16[256,512]{0,1:T(8,128)(2,1)}), bf16[2048,512]{0,1:T(8,128)(2,1)}) %all-gather.7.cloned.1.call-update) | async-done | bytes 2097168 | tf_op jit(solution)/shard_map/all_gather | solution.py:92
  63.1 67.7 %all-gather.5.cloned.1.call-done = bf16[1536,2048]{1,0:T(8,128)(2,1)} async-done(((bf16[96,2048]{1,0:T(8,128)(2,1)}), bf16[1536,2048]{1,0:T(8,128)(2,1)}) %all-gather.5.cloned.1.call-update) | async-done | bytes 6291472 | tf_op jit(solution)/shard_map/all_gather | solution.py:83
  130.8 5.2 fusion.10
  136.0 3.3 fusion.13
  139.3 1.7 fusion.62
  141.0 3.3 fusion.11
  145.3 3.6 collective-permute-start.2
  149.3 8.4 %collective-permute-done.2 = bf16[512,1,2,128]{0,3,2,1:T(8,128)(2,1)S(1)} collective-permute-done((bf16[512,1,2,128]{0,3,2,1:T(8,128)(2,1)S(1)}, bf16[512,1,2,128]{0,3,2,1:T(8,128)(2,1)S(1)}, u32[]{:S(2)}, u32[]{:S(2)}) %collective-permute-start.2) | collective-permute-done | bytes 262176 | tf_op jit(solution)/shard_map/ppermute | solution.py:26
  157.9 3.0 fusion
  160.8 4.5 copy-done
  165.4 4.5 fusion.1
  169.8 10.8 %convolution_convert_fusion.1 = bf16[1536,2048]{1,0:T(8,128)(2,1)} fusion(f32[1536,2048]{1,0:T(8,128)} %copy-done, f32[1536]{0:T(1024)S(1)} %get-tuple-element.10, bf16[2048,512]{0,1:T(8,128)(2,1)} %all-gather.7.cloned.1.call-done, bf16[2048,1,2,128]{0,3,2,1:T(8,128)(2,1)} %copy-done.5, f32[1536]{0:T(1024)S(1)} %fusion.1, ...), kind=kOutput, calls=%fused_computation.7 | convolution fusion | flops 1633026048 | bytes 23080960 | tf_op jit(solution)/shard_map/dot_general | solution.py:56
  180.7 0.9 copy-done.6
  182.0 0.9 pad_maximum_fusion.1
  183.0 83.1 %reduce-scatter.3.cloned.1.call-done = bf16[96,2048]{1,0:T(8,128)(2,1)} async-done(((bf16[1536,2048]{1,0:T(8,128)(2,1)}), bf16[96,2048]{1,0:T(8,128)(2,1)}) %reduce-scatter.3.cloned.1.call-update) | async-done | bytes 393232 | tf_op jit(solution)/shard_map/reduce_scatter | solution.py:136
  266.1 1.2 multiply_reduce_fusion
  267.4 1.9 multiply_convert_fusion
  269.6 76.9 %all-gather.11.cloned.1.call-done = bf16[2048,1536]{0,1:T(8,128)(2,1)} async-done(((bf16[256,1536]{0,1:T(8,128)(2,1)}), bf16[2048,1536]{0,1:T(8,128)(2,1)}) %all-gather.11.cloned.1.call-update) | async-done | bytes 6291472 | tf_op jit(solution)/shard_map/all_gather | solution.py:99
  346.5 67.5 %all-gather.9.cloned.1.call-done = bf16[1536,2048]{1,0:T(8,128)(2,1)} async-done(((bf16[96,2048]{1,0:T(8,128)(2,1)}), bf16[1536,2048]{1,0:T(8,128)(2,1)}) %all-gather.9.cloned.1.call-update) | async-done | bytes 6291472 | tf_op jit(solution)/shard_map/all_gather | solution.py:138
  414.0 8.6 %fusion.25 = f32[1536,512]{1,0:T(8,128)} fusion(bf16[1536,2048]{1,0:T(8,128)(2,1)} %all-gather.9.cloned.1.call-done, bf16[2048,1536]{0,1:T(8,128)(2,1)} %all-gather.11.cloned.1.call-done), kind=kOutput, calls=%fused_computation.27 | convolution fusion | flops 3221225472 | bytes 11534336 | tf_op jit(solution)/shard_map/dot_general | solution.py:139
  422.5 12.4 %convolution_convert_fusion = bf16[1536,2048]{1,0:T(8,128)(2,1)} fusion(bf16[2048,1536]{0,1:T(8,128)(2,1)} %all-gather.11.cloned.1.call-done, bf16[1536,2048]{1,0:T(8,128)(2,1)} %all-gather.9.cloned.1.call-done, f32[1536,512]{1,0:T(8,128)} %fusion.25), kind=kOutput, calls=%fused_computation.6 | convolution fusion | flops 6450315264 | bytes 19922944 | tf_op jit(solution)/shard_map/dot_general | solution.py:56
  435.0 1.1 copy-done.4
  436.3 6.1 %scatter_custom_fusion = bf16[8192,128]{1,0:T(8,128)(2,1)} fusion(s32[1536]{0:T(1024)S(1)} %get-tuple-element.8, bf16[1536,128]{1,0:T(8,128)(2,1)S(1)} %copy.26, bf16[]{:T(256)} %constant.81.clone.1), kind=kCustom, calls=%fused_computation.34 | custom fusion | bytes 2097154 | tf_op jit(solution)/shard_map/scatter | solution.py:159
  442.4 80.1 %reduce-scatter.5.cloned.1.call-done = bf16[96,2048]{1,0:T(8,128)(2,1)} async-done(((bf16[1536,2048]{1,0:T(8,128)(2,1)}), bf16[96,2048]{1,0:T(8,128)(2,1)}) %reduce-scatter.5.cloned.1.call-update) | async-done | bytes 393232 | tf_op jit(solution)/shard_map/reduce_scatter | solution.py:143
  522.6 1.9 add_convert_fusion
  (73 shorter events, 11.2 us)
Async XLA Ops:
  7.2 16.3 %copy-start.10 = (s32[1536]{0:T(1024)S(1)}, s32[1536]{0:T(1024)}, u32[]{:S(2)}) copy-start(s32[1536]{0:T(1024)} %param.14) | copy-start | bytes 18436
  7.2 14.8 %copy-start.11 = (s32[1536]{0:T(1024)S(1)}, s32[1536]{0:T(1024)}, u32[]{:S(2)}) copy-start(s32[1536]{0:T(1024)} %param.15) | copy-start | bytes 18436
  7.2 16.1 %copy-start.13 = (s32[1,64]{1,0:T(1,128)S(1)}, s32[1,64]{1,0:T(1,128)}, u32[]{:S(2)}) copy-start(s32[1,64]{1,0:T(1,128)} %param.16) | copy-start | bytes 772
  7.2 55.9 %all-gather.7.cloned.1.call-start = ((), (), s32[]{:S(2)}) async-start(), calls=%async_computation.3 | async-start | bytes 2359296 | tf_op jit(solution)/shard_map/all_gather | solution.py:92
  8.1 2.4 collective-permute-start
  8.9 3.3 collective-permute-start.1
  14.8 0.7 copy-start.9
  15.5 115.2 %all-gather.5.cloned.1.call-start = ((), (), s32[]{:S(2)}) async-start(), calls=%async_computation.2 | async-start | bytes 6684672 | tf_op jit(solution)/shard_map/all_gather | solution.py:83
  18.7 247.4 %reduce-scatter.3.cloned.1.call-start = ((), (), s32[]{:S(2)}) async-start(), calls=%async_computation.4 | async-start | bytes 6684672 | tf_op jit(solution)/shard_map/reduce_scatter | solution.py:136
  130.7 5.2 copy-start.14
  144.4 0.9 copy-start.3
  145.3 12.5 %collective-permute-start.2 = (bf16[512,1,2,128]{0,3,2,1:T(8,128)(2,1)S(1)}, bf16[512,1,2,128]{0,3,2,1:T(8,128)(2,1)S(1)}, u32[]{:S(2)}, u32[]{:S(2)}) collective-permute-start(bf16[512,1,2,128]{0,3,2,1:T(8,128)(2,1)S(1)} %slice.87), channel_id=1, source_target_pairs={{0,16},{16,32},{32,48},{48,64},{64,80},{80,96},{96,112},{1,17},{17... | collective-permute-start | bytes 786440 | tf_op jit(solution)/shard_map/ppermute | solution.py:26
  157.8 3.0 copy-start.5
  160.8 4.5 copy-start
  180.6 1.0 copy-start.6
  180.6 1.2 copy-start.7
  180.6 1.4 copy-start.8
  180.7 85.5 %copy-start.1 = (bf16[96,2048]{1,0:T(8,128)(2,1)S(1)}, bf16[96,2048]{1,0:T(8,128)(2,1)}, u32[]{:S(2)}) copy-start(bf16[96,2048]{1,0:T(8,128)(2,1)} %param.13) | copy-start | bytes 1179652
  180.7 86.7 %copy-start.12 = (f32[2048]{0:T(1024)S(1)}, f32[2048]{0:T(1024)}, u32[]{:S(2)}) copy-start(f32[2048]{0:T(1024)} %param.18) | copy-start | bytes 24580
  180.7 165.8 %all-gather.11.cloned.1.call-start = ((), (), s32[]{:S(2)}) async-start(), calls=%async_computation.6 | async-start | bytes 7077888 | tf_op jit(solution)/shard_map/all_gather | solution.py:99
  183.0 231.0 %all-gather.9.cloned.1.call-start = ((), (), s32[]{:S(2)}) async-start(), calls=%async_computation.5 | async-start | bytes 6684672 | tf_op jit(solution)/shard_map/all_gather | solution.py:138
  269.3 253.3 %reduce-scatter.5.cloned.1.call-start = ((), (), s32[]{:S(2)}) async-start(), calls=%async_computation.7 | async-start | bytes 6684672 | tf_op jit(solution)/shard_map/reduce_scatter | solution.py:143
  434.9 1.1 copy-start.4
  435.0 87.6 %copy-start.2 = (bf16[96,2048]{1,0:T(8,128)(2,1)S(1)}, bf16[96,2048]{1,0:T(8,128)(2,1)}, u32[]{:S(2)}) copy-start(bf16[96,2048]{1,0:T(8,128)(2,1)} %reduce-scatter.3.cloned.1.call-done) | copy-start | bytes 1179652
Sparse Core Ops, SparseCore 0:
  15.7 47.3 all-gather.6
  66.1 64.5 all-gather.4
  180.8 85.3 reduce-scatter.2
  268.2 78.2 all-gather.10
  349.7 64.1 all-gather.8
  435.1 87.4 reduce-scatter.4

commit v2 on v1

--- a/solution.py
+++ b/solution.py
@@ -24,6 +24,17 @@
     devices = range(lax.axis_size(axis))
     route = [(i - distance, i) for i in devices if i - distance in devices]
     return lax.ppermute(block, axis, route)
+
+
+def gather_group(block):
+    count = lax.axis_size("group")
+    pieces = [block]
+    for shift in range(1, count):
+        route = [(source, (source + shift) % count) for source in range(count)]
+        pieces.append(lax.ppermute(block, "group", route))
+    stacked = jnp.stack(pieces)
+    order = (lax.axis_index("group") - jnp.arange(count)) % count
+    return jnp.take(stacked, order, axis=0).reshape(count * block.shape[0], block.shape[1])
 
 
 def rms_scale(values, gain):
@@ -89,14 +100,14 @@
     q_cols = query_heads * HD
     kv_cols = key_heads * HD
     attn_w = jnp.concatenate([wq.astype(bf), key_rows, value_rows, wo.astype(bf).T], axis=1)
-    attn_w = lax.all_gather(attn_w, "group", axis=0, tiled=True)
+    attn_w = gather_group(attn_w)
     query_w = attn_w[:, :q_cols]
     key_w = attn_w[:, q_cols : q_cols + kv_cols]
     value_w = attn_w[:, q_cols + kv_cols : q_cols + 2 * kv_cols]
     out_w_t = attn_w[:, q_cols + 2 * kv_cols :]
     ff_cols = w_gate.shape[1]
     mlp_w = jnp.concatenate([w_gate.astype(bf), w_up.astype(bf), w_down.astype(bf).T], axis=1)
-    mlp_w = lax.all_gather(mlp_w, "group", axis=0, tiled=True)
+    mlp_w = gather_group(mlp_w)
     gate_w = mlp_w[:, :ff_cols]
     up_w = mlp_w[:, ff_cols : 2 * ff_cols]
     down_w_t = mlp_w[:, 2 * ff_cols :]

time: 533 us -> 468 us (0.88)
  waiting for transfers between devices: 420 us -> 288 us
  starting transfers between devices: 4.61 us -> 46.5 us
  local copies, waits for them, and re-layouts: 18.4 us -> 39.5 us
  other arithmetic: 26.3 us -> 33.2 us
    all_gather x2 -> x0, waiting for transfers between devices: 114 us -> none  [the longest x1 76.9 us: body(): mlp_w = lax.all_gather(mlp_w, 'group', axis=0, tiled=True)]
    ppermute x0 -> x14, waiting for transfers between devices: none -> 93.4 us  [gather_group(): pieces.append(lax.ppermute(block, 'group', route))]
    all_gather x1, waiting for transfers between devices: 67.5 us -> 0.01 us  [body(): lax.all_gather(rms_scale(mixed, mlp_gain), 'tensor', axis=0, tiled=True)]
    all_gather x1, waiting for transfers between devices: 67.7 us -> 13.4 us  [body(): lax.all_gather(rms_scale(residual, attn_gain), 'tensor', axis=0, tiled=True)]
    ppermute x0 -> x14, starting transfers between devices: none -> 42.8 us  [gather_group(): pieces.append(lax.ppermute(block, 'group', route))]
    gather x0 -> x2, local copies, waits for them, and re-layouts: none -> 9.99 us  [gather_group(): jnp.take(stacked, order, axis=0)]
    unnamed x35 -> x46, local copies, waits for them, and re-layouts: 9.68 us -> 18.9 us
    select_n x0 -> x5, other arithmetic: none -> 8.83 us  [the longest x3 8.8 us: gather_group(): jnp.take(stacked, order, axis=0)]
  transfers between devices with their start and end apart: 9 -> 21, of which waited for: 7 -> 12; matrix products, arithmetic and copies ran while one was open for 5% -> 11% of each run, Pallas kernels for 0% -> 0%
where the time goes in v2:
time: 468 us; the launch traced here: 466 us
  waiting for transfers between devices  288 us (62%)
  starting transfers between devices  46.5 us (10%)
  matrix products  44.1 us (9%)
  local copies, waits for them, and re-layouts  39.5 us (8%)
  other arithmetic  33.2 us (7%)
  between operations  14.8 us (3%)
    ppermute x14, waiting for transfers between devices, gather_group(): pieces.append(lax.ppermute(block, 'group', route))  93.4 us
    reduce_scatter x1, waiting for transfers between devices, body(): lax.psum_scatter(attn_part.astype(bf), 'tensor', scatter_dimension=0, til...  85.7 us
    reduce_scatter x1, waiting for transfers between devices, body(): lax.psum_scatter(down_part.astype(bf), 'tensor', scatter_dimension=0, til...  85.1 us
    ppermute x14, starting transfers between devices, gather_group(): pieces.append(lax.ppermute(block, 'group', route))  42.8 us
    dot_general x2, matrix products, dot_t(): lax.dot_general(acts, weight_t, (((1,), (1,)), ((), ())), preferred_eleme...  23 us
    unnamed x46, local copies, waits for them, and re-layouts  18.9 us
    all_gather x1, waiting for transfers between devices, body(): lax.all_gather(rms_scale(residual, attn_gain), 'tensor', axis=0, tiled=True)  13.4 us
    ppermute x1, waiting for transfers between devices, from_behind(): return lax.ppermute(block, axis, route)  10.4 us
  transfers between devices with their start and end apart: 21, of which 12 were waited for; matrix products, arithmetic and copies ran while one was open for 11% of the time, Pallas kernels for 0%

profile of v2, /device:TPU:2, one launch (start us, length us, event | category | flops | bytes accessed | tf_op | source)
XLA Modules:
  0.0 466.4 jit_solution(4436823099612955865)
XLA Ops:
  19.4 3.3 compare_and_fusion
  25.0 2.0 collective-permute-start.2
  27.1 3.6 collective-permute-start.3
  34.9 7.5 %collective-permute-done.2 = bf16[256,512]{1,0:T(8,128)(2,1)S(1)} collective-permute-done((bf16[256,512]{1,0:T(8,128)(2,1)S(1)}, bf16[256,512]{1,0:T(8,128)(2,1)S(1)}, u32[]{:S(2)}, u32[]{:S(2)}) %collective-permute-start.2) | collective-permute-done | bytes 262176 | tf_op jit(solution)/shard_map/ppermute | solution.py:34
  43.4 6.2 %collective-permute-start.8 = (bf16[256,512]{1,0:T(8,128)(2,1)S(1)}, bf16[256,512]{1,0:T(8,128)(2,1)S(1)}, u32[]{:S(2)}, u32[]{:S(2)}) collective-permute-start(bf16[256,512]{1,0:T(8,128)(2,1)S(1)} %concatenate.46), channel_id=1, source_target_pairs={{0,112},{16,0},{32,16},{48,32},{64,48},{80,64},{96,80},{112,96},{1... | collective-permute-start | bytes 786440 | tf_op jit(solution)/shard_map/ppermute | solution.py:34
  56.9 8.7 %collective-permute-done.8 = bf16[256,512]{1,0:T(8,128)(2,1)S(1)} collective-permute-done((bf16[256,512]{1,0:T(8,128)(2,1)S(1)}, bf16[256,512]{1,0:T(8,128)(2,1)S(1)}, u32[]{:S(2)}, u32[]{:S(2)}) %collective-permute-start.8) | collective-permute-done | bytes 262176 | tf_op jit(solution)/shard_map/ppermute | solution.py:34
  66.3 3.6 gather_fusion
  69.9 2.7 bitcast_select_fusion.1
  72.6 13.4 %all-gather.3.cloned.1.call-done = bf16[1536,2048]{1,0:T(8,128)(2,1)} async-done(((bf16[96,2048]{1,0:T(8,128)(2,1)}), bf16[1536,2048]{1,0:T(8,128)(2,1)}) %all-gather.3.cloned.1.call-update) | async-done | bytes 6291472 | tf_op jit(solution)/shard_map/all_gather | solution.py:94
  86.0 5.2 %fusion.10 = f32[1536,1,128]{0,2,1:T(8,128)S(1)} fusion(bf16[1536,2048]{1,0:T(8,128)(2,1)} %all-gather.3.cloned.1.call-done, bf16[2048,512]{1,0:T(8,128)(2,1)} %bitcast_select_fusion.1), kind=kOutput, calls=%fused_computation.21 | convolution fusion | flops 805699584 | bytes 7602176 | tf_op jit(solution)/shard_map/dot_general | solution.py:115
  91.4 2.2 fusion.13
  95.4 2.2 fusion.11
  97.7 2.9 collective-permute-start.9
  101.0 10.4 %collective-permute-done.9 = bf16[512,1,2,128]{0,3,2,1:T(8,128)(2,1)S(1)} collective-permute-done((bf16[512,1,2,128]{0,3,2,1:T(8,128)(2,1)S(1)}, bf16[512,1,2,128]{0,3,2,1:T(8,128)(2,1)S(1)}, u32[]{:S(2)}, u32[]{:S(2)}) %collective-permute-start.9) | collective-permute-done | bytes 262176 | tf_op jit(solution)/shard_map/ppermute | solution.py:26
  111.6 2.9 fusion
  114.5 4.5 copy-done.1
  119.0 4.5 fusion.1
  123.5 10.7 %convolution_convert_fusion.1 = bf16[1536,2048]{1,0:T(8,128)(2,1)} fusion(f32[1536,2048]{1,0:T(8,128)} %copy-done.1, f32[1536]{0:T(1024)S(1)} %get-tuple-element.14, bf16[2048,512]{1,0:T(8,128)(2,1)} %bitcast_select_fusion.1, bf16[2048,1,2,128]{0,3,2,1:T(8,128)(2,1)} %copy-done.7, f32[1536]{0:T(1024)S(1)} %fusion.1, ...), kind=kOutput, calls=%fused_computation.9 | convolution fusion | flops 1633026048 | bytes 23080960 | tf_op jit(solution)/shard_map/dot_general | solution.py:67
  134.3 85.7 %reduce-scatter.3.cloned.1.call-done = bf16[96,2048]{1,0:T(8,128)(2,1)} async-done(((bf16[1536,2048]{1,0:T(8,128)(2,1)}), bf16[96,2048]{1,0:T(8,128)(2,1)}) %reduce-scatter.3.cloned.1.call-update) | async-done | bytes 393232 | tf_op jit(solution)/shard_map/reduce_scatter | solution.py:147
  225.3 2.8 collective-permute-start.11
  228.1 2.3 collective-permute-start.12
  233.5 27.4 %collective-permute-done.10 = bf16[256,1536]{1,0:T(8,128)(2,1)S(1)} collective-permute-done((bf16[256,1536]{1,0:T(8,128)(2,1)S(1)}, bf16[256,1536]{1,0:T(8,128)(2,1)S(1)}, u32[]{:S(2)}, u32[]{:S(2)}) %collective-permute-start.10) | collective-permute-done | bytes 786464 | tf_op jit(solution)/shard_map/ppermute | solution.py:34
  262.6 12.7 %collective-permute-done.11 = bf16[256,1536]{1,0:T(8,128)(2,1)S(1)} collective-permute-done((bf16[256,1536]{1,0:T(8,128)(2,1)S(1)}, bf16[256,1536]{1,0:T(8,128)(2,1)S(1)}, u32[]{:S(2)}, u32[]{:S(2)}) %collective-permute-start.11) | collective-permute-done | bytes 786464 | tf_op jit(solution)/shard_map/ppermute | solution.py:34
  275.3 17.6 %collective-permute-start.16 = (bf16[256,1536]{1,0:T(8,128)(2,1)S(1)}, bf16[256,1536]{1,0:T(8,128)(2,1)S(1)}, u32[]{:S(2)}, u32[]{:S(2)}) collective-permute-start(bf16[256,1536]{1,0:T(8,128)(2,1)S(1)} %pad_maximum_fusion.1), channel_id=1, source_target_pairs={{0,112},{16,0},{32,16},{48,32},{64,48},{80,64},{96,80},{112,96},{1... | collective-permute-start | bytes 2359304 | tf_op jit(solution)/shard_map/ppermute | solution.py:34
  296.7 7.0 %collective-permute-done.15 = bf16[256,1536]{1,0:T(8,128)(2,1)S(1)} collective-permute-done((bf16[256,1536]{1,0:T(8,128)(2,1)S(1)}, bf16[256,1536]{1,0:T(8,128)(2,1)S(1)}, u32[]{:S(2)}, u32[]{:S(2)}) %collective-permute-start.15) | collective-permute-done | bytes 786464 | tf_op jit(solution)/shard_map/ppermute | solution.py:34
  304.7 26.4 %collective-permute-done.16 = bf16[256,1536]{1,0:T(8,128)(2,1)S(1)} collective-permute-done((bf16[256,1536]{1,0:T(8,128)(2,1)S(1)}, bf16[256,1536]{1,0:T(8,128)(2,1)S(1)}, u32[]{:S(2)}, u32[]{:S(2)}) %collective-permute-start.16) | collective-permute-done | bytes 786464 | tf_op jit(solution)/shard_map/ppermute | solution.py:34
  332.1 6.4 %gather_fusion.1 = bf16[8,256,1536]{2,1,0:T(8,128)(2,1)} fusion(bf16[8,256,1536]{2,1,0:T(8,128)(2,1)} %bitcast_dynamic-update-slice_fusion, s32[1024]{0:T(1024)S(1)} %pad_clamp_fusion), kind=kCustom, calls=%fused_computation.1 | custom fusion | bytes 12582944 | tf_op jit(solution)/shard_map/jit(_take)/gather | solution.py:37
  338.4 6.0 %bitcast_select_fusion = bf16[2048,1536]{1,0:T(8,128)(2,1)} fusion(bf16[8,256,1536]{2,1,0:T(8,128)(2,1)} %gather_fusion.1, pred[2048]{0:T(1024)(128)(4,1)S(1)} %broadcast_in_dim.77), kind=kLoop, calls=%fused_computation.12 | loop fusion | flops 3145728 | bytes 12584960 | tf_op jit(solution)/shard_map/jit(_take)/select_n | solution.py:37
  344.5 8.5 %fusion.25 = f32[1536,512]{1,0:T(8,128)} fusion(bf16[1536,2048]{1,0:T(8,128)(2,1)} %all-gather.5.cloned.1.call-done, bf16[2048,1536]{1,0:T(8,128)(2,1)} %bitcast_select_fusion), kind=kOutput, calls=%fused_computation.30 | convolution fusion | flops 3221225472 | bytes 11534336 | tf_op jit(solution)/shard_map/dot_general | solution.py:150
  353.0 12.3 %convolution_convert_fusion = bf16[1536,2048]{1,0:T(8,128)(2,1)} fusion(bf16[2048,1536]{1,0:T(8,128)(2,1)} %bitcast_select_fusion, bf16[1536,2048]{1,0:T(8,128)(2,1)} %all-gather.5.cloned.1.call-done, f32[1536,512]{1,0:T(8,128)} %fusion.25), kind=kOutput, calls=%fused_computation.8 | convolution fusion | flops 6450315264 | bytes 19922944 | tf_op jit(solution)/shard_map/dot_general | solution.py:67
  366.7 6.1 %scatter_custom_fusion = bf16[8192,128]{1,0:T(8,128)(2,1)} fusion(s32[1536]{0:T(1024)S(1)} %get-tuple-element.12, bf16[1536,128]{1,0:T(8,128)(2,1)S(1)} %copy.32, bf16[]{:T(256)} %constant.130.clone.1), kind=kCustom, calls=%fused_computation.38 | custom fusion | bytes 2097154 | tf_op jit(solution)/shard_map/scatter | solution.py:170
  372.8 85.1 %reduce-scatter.5.cloned.1.call-done = bf16[96,2048]{1,0:T(8,128)(2,1)} async-done(((bf16[1536,2048]{1,0:T(8,128)(2,1)}), bf16[96,2048]{1,0:T(8,128)(2,1)}) %reduce-scatter.5.cloned.1.call-update) | async-done | bytes 393232 | tf_op jit(solution)/shard_map/reduce_scatter | solution.py:154
  (116 shorter events, 48.4 us)
Async XLA Ops:
  7.2 16.8 %copy-start.11 = (f32[128,256]{1,0:T(8,128)S(1)}, f32[128,256]{1,0:T(8,128)}, u32[]{:S(2)}) copy-start(f32[128,256]{1,0:T(8,128)} %param.22) | copy-start | bytes 393220
  7.2 16.9 %copy-start.12 = (f32[256,128]{1,0:T(8,128)S(1)}, f32[256,128]{1,0:T(8,128)}, u32[]{:S(2)}) copy-start(f32[256,128]{1,0:T(8,128)} %param.19) | copy-start | bytes 393220
  7.2 78.9 %all-gather.3.cloned.1.call-start = ((), (), s32[]{:S(2)}) async-start(), calls=%async_computation.2 | async-start | bytes 6684672 | tf_op jit(solution)/shard_map/all_gather | solution.py:94
  10.4 209.7 %reduce-scatter.3.cloned.1.call-start = ((), (), s32[]{:S(2)}) async-start(), calls=%async_computation.3 | async-start | bytes 6684672 | tf_op jit(solution)/shard_map/reduce_scatter | solution.py:147
  11.4 13.4 %collective-permute-start.1 = (bf16[256,64]{1,0:T(8,128)(2,1)S(1)}, bf16[256,64]{1,0:T(8,128)(2,1)S(1)}, u32[]{:S(2)}, u32[]{:S(2)}) collective-permute-start(bf16[256,64]{1,0:T(8,128)(2,1)S(1)} %copy.28), channel_id=1, source_target_pairs={{0,1},{1,0},{2,3},{3,2},{4,5},{5,4},{6,7},{7,6},{8,9},{9,8},{10,11... | collective-permute-start | bytes 98312 | tf_op jit(solution)/shard_map/ppermute | solution.py:20
  12.5 12.3 %collective-permute-start = (bf16[256,64]{1,0:T(8,128)(2,1)S(1)}, bf16[256,64]{1,0:T(8,128)(2,1)S(1)}, u32[]{:S(2)}, u32[]{:S(2)}) collective-permute-start(bf16[256,64]{1,0:T(8,128)(2,1)S(1)} %copy.27), channel_id=1, source_target_pairs={{0,1},{1,0},{2,3},{3,2},{4,5},{5,4},{6,7},{7,6},{8,9},{9,8},{10,11... | collective-permute-start | bytes 98312 | tf_op jit(solution)/shard_map/ppermute | solution.py:20
  25.0 17.4 %collective-permute-start.2 = (bf16[256,512]{1,0:T(8,128)(2,1)S(1)}, bf16[256,512]{1,0:T(8,128)(2,1)S(1)}, u32[]{:S(2)}, u32[]{:S(2)}) collective-permute-start(bf16[256,512]{1,0:T(8,128)(2,1)S(1)} %concatenate.46), channel_id=1, source_target_pairs={{0,16},{16,32},{32,48},{48,64},{64,80},{80,96},{96,112},{112,0},{1... | collective-permute-start | bytes 786440 | tf_op jit(solution)/shard_map/ppermute | solution.py:34
  27.1 16.3 %collective-permute-start.3 = (bf16[256,512]{1,0:T(8,128)(2,1)S(1)}, bf16[256,512]{1,0:T(8,128)(2,1)S(1)}, u32[]{:S(2)}, u32[]{:S(2)}) collective-permute-start(bf16[256,512]{1,0:T(8,128)(2,1)S(1)} %concatenate.46), channel_id=1, source_target_pairs={{0,32},{16,48},{32,64},{48,80},{64,96},{80,112},{96,0},{112,16},{1... | collective-permute-start | bytes 786440 | tf_op jit(solution)/shard_map/ppermute | solution.py:34
  31.4 18.8 %collective-permute-start.4 = (bf16[256,512]{1,0:T(8,128)(2,1)S(1)}, bf16[256,512]{1,0:T(8,128)(2,1)S(1)}, u32[]{:S(2)}, u32[]{:S(2)}) collective-permute-start(bf16[256,512]{1,0:T(8,128)(2,1)S(1)} %concatenate.46), channel_id=1, source_target_pairs={{0,48},{16,64},{32,80},{48,96},{64,112},{80,0},{96,16},{112,32},{1... | collective-permute-start | bytes 786440 | tf_op jit(solution)/shard_map/ppermute | solution.py:34
  32.4 18.6 %collective-permute-start.5 = (bf16[256,512]{1,0:T(8,128)(2,1)S(1)}, bf16[256,512]{1,0:T(8,128)(2,1)S(1)}, u32[]{:S(2)}, u32[]{:S(2)}) collective-permute-start(bf16[256,512]{1,0:T(8,128)(2,1)S(1)} %concatenate.46), channel_id=1, source_target_pairs={{0,64},{16,80},{32,96},{48,112},{64,0},{80,16},{96,32},{112,48},{1... | collective-permute-start | bytes 786440 | tf_op jit(solution)/shard_map/ppermute | solution.py:34
  33.9 19.6 %collective-permute-start.6 = (bf16[256,512]{1,0:T(8,128)(2,1)S(1)}, bf16[256,512]{1,0:T(8,128)(2,1)S(1)}, u32[]{:S(2)}, u32[]{:S(2)}) collective-permute-start(bf16[256,512]{1,0:T(8,128)(2,1)S(1)} %concatenate.46), channel_id=1, source_target_pairs={{0,80},{16,96},{32,112},{48,0},{64,16},{80,32},{96,48},{112,64},{1... | collective-permute-start | bytes 786440 | tf_op jit(solution)/shard_map/ppermute | solution.py:34
  42.4 13.7 %collective-permute-start.7 = (bf16[256,512]{1,0:T(8,128)(2,1)S(1)}, bf16[256,512]{1,0:T(8,128)(2,1)S(1)}, u32[]{:S(2)}, u32[]{:S(2)}) collective-permute-start(bf16[256,512]{1,0:T(8,128)(2,1)S(1)} %concatenate.46), channel_id=1, source_target_pairs={{0,96},{16,112},{32,0},{48,16},{64,32},{80,48},{96,64},{112,80},{1... | collective-permute-start | bytes 786440 | tf_op jit(solution)/shard_map/ppermute | solution.py:34
  43.4 22.2 %collective-permute-start.8 = (bf16[256,512]{1,0:T(8,128)(2,1)S(1)}, bf16[256,512]{1,0:T(8,128)(2,1)S(1)}, u32[]{:S(2)}, u32[]{:S(2)}) collective-permute-start(bf16[256,512]{1,0:T(8,128)(2,1)S(1)} %concatenate.46), channel_id=1, source_target_pairs={{0,112},{16,0},{32,16},{48,32},{64,48},{80,64},{96,80},{112,96},{1... | collective-permute-start | bytes 786440 | tf_op jit(solution)/shard_map/ppermute | solution.py:34
  86.0 5.2 %copy-start = (bf16[1536,2048]{1,0:T(8,128)(2,1)S(1)}, bf16[1536,2048]{1,0:T(8,128)(2,1)}, u32[]{:S(2)}) copy-start(bf16[1536,2048]{1,0:T(8,128)(2,1)} %all-gather.3.cloned.1.call-done) | copy-start | bytes 18874372
  86.0 5.4 %copy-start.3 = (bf16[2048,512]{1,0:T(8,128)(2,1)S(1)}, bf16[2048,512]{1,0:T(8,128)(2,1)}, u32[]{:S(2)}) copy-start(bf16[2048,512]{1,0:T(8,128)(2,1)} %bitcast_select_fusion.1) | copy-start | bytes 6291460
  97.7 13.9 %copy-start.5 = (bf16[1536,1,2,128]{0,3,2,1:T(8,128)(2,1)}, bf16[1536,1,2,128]{0,3,2,1:T(8,128)(2,1)S(1)}, u32[]{:S(2)}) copy-start(bf16[1536,1,2,128]{0,3,2,1:T(8,128)(2,1)S(1)} %pad_maximum_fusion) | copy-start | bytes 2359300
  97.7 13.7 %collective-permute-start.9 = (bf16[512,1,2,128]{0,3,2,1:T(8,128)(2,1)S(1)}, bf16[512,1,2,128]{0,3,2,1:T(8,128)(2,1)S(1)}, u32[]{:S(2)}, u32[]{:S(2)}) collective-permute-start(bf16[512,1,2,128]{0,3,2,1:T(8,128)(2,1)S(1)} %slice.91), channel_id=1, source_target_pairs={{0,16},{16,32},{32,48},{48,64},{64,80},{80,96},{96,112},{1,17},{17... | collective-permute-start | bytes 786440 | tf_op jit(solution)/shard_map/ppermute | solution.py:26
  134.2 85.8 %copy-start.2 = (bf16[96,2048]{1,0:T(8,128)(2,1)S(1)}, bf16[96,2048]{1,0:T(8,128)(2,1)}, u32[]{:S(2)}) copy-start(bf16[96,2048]{1,0:T(8,128)(2,1)} %param.13) | copy-start | bytes 1179652
  134.2 87.1 %copy-start.13 = (f32[2048]{0:T(1024)S(1)}, f32[2048]{0:T(1024)}, u32[]{:S(2)}) copy-start(f32[2048]{0:T(1024)} %param.18) | copy-start | bytes 24580
  134.2 89.1 %copy-start.8 = (f32[512,256]{1,0:T(8,128)S(1)}, f32[512,256]{1,0:T(8,128)}, u32[]{:S(2)}) copy-start(f32[512,256]{1,0:T(8,128)} %param.25) | copy-start | bytes 1572868
  134.3 89.2 %copy-start.9 = (f32[256,512]{1,0:T(8,128)S(1)}, f32[256,512]{1,0:T(8,128)}, u32[]{:S(2)}) copy-start(f32[256,512]{1,0:T(8,128)} %param.23) | copy-start | bytes 1572868
  134.3 89.2 %copy-start.10 = (f32[256,512]{1,0:T(8,128)S(1)}, f32[256,512]{1,0:T(8,128)}, u32[]{:S(2)}) copy-start(f32[256,512]{1,0:T(8,128)} %param.24) | copy-start | bytes 1572868
  134.3 210.2 %all-gather.5.cloned.1.call-start = ((), (), s32[]{:S(2)}) async-start(), calls=%async_computation.4 | async-start | bytes 6684672 | tf_op jit(solution)/shard_map/all_gather | solution.py:149
  223.3 234.7 %reduce-scatter.5.cloned.1.call-start = ((), (), s32[]{:S(2)}) async-start(), calls=%async_computation.5 | async-start | bytes 6684672 | tf_op jit(solution)/shard_map/reduce_scatter | solution.py:154
  223.6 37.2 %collective-permute-start.10 = (bf16[256,1536]{1,0:T(8,128)(2,1)S(1)}, bf16[256,1536]{1,0:T(8,128)(2,1)S(1)}, u32[]{:S(2)}, u32[]{:S(2)}) collective-permute-start(bf16[256,1536]{1,0:T(8,128)(2,1)S(1)} %pad_maximum_fusion.1), channel_id=1, source_target_pairs={{0,16},{16,32},{32,48},{48,64},{64,80},{80,96},{96,112},{112,0},{1... | collective-permute-start | bytes 2359304 | tf_op jit(solution)/shard_map/ppermute | solution.py:34
  225.3 50.0 %collective-permute-start.11 = (bf16[256,1536]{1,0:T(8,128)(2,1)S(1)}, bf16[256,1536]{1,0:T(8,128)(2,1)S(1)}, u32[]{:S(2)}, u32[]{:S(2)}) collective-permute-start(bf16[256,1536]{1,0:T(8,128)(2,1)S(1)} %pad_maximum_fusion.1), channel_id=1, source_target_pairs={{0,32},{16,48},{32,64},{48,80},{64,96},{80,112},{96,0},{112,16},{1... | collective-permute-start | bytes 2359304 | tf_op jit(solution)/shard_map/ppermute | solution.py:34
  228.1 65.8 %collective-permute-start.12 = (bf16[256,1536]{1,0:T(8,128)(2,1)S(1)}, bf16[256,1536]{1,0:T(8,128)(2,1)S(1)}, u32[]{:S(2)}, u32[]{:S(2)}) collective-permute-start(bf16[256,1536]{1,0:T(8,128)(2,1)S(1)} %pad_maximum_fusion.1), channel_id=1, source_target_pairs={{0,48},{16,64},{32,80},{48,96},{64,112},{80,0},{96,16},{112,32},{1... | collective-permute-start | bytes 2359304 | tf_op jit(solution)/shard_map/ppermute | solution.py:34
  230.4 64.5 %collective-permute-start.13 = (bf16[256,1536]{1,0:T(8,128)(2,1)S(1)}, bf16[256,1536]{1,0:T(8,128)(2,1)S(1)}, u32[]{:S(2)}, u32[]{:S(2)}) collective-permute-start(bf16[256,1536]{1,0:T(8,128)(2,1)S(1)} %pad_maximum_fusion.1), channel_id=1, source_target_pairs={{0,64},{16,80},{32,96},{48,112},{64,0},{80,16},{96,32},{112,48},{1... | collective-permute-start | bytes 2359304 | tf_op jit(solution)/shard_map/ppermute | solution.py:34
  230.9 64.8 %collective-permute-start.14 = (bf16[256,1536]{1,0:T(8,128)(2,1)S(1)}, bf16[256,1536]{1,0:T(8,128)(2,1)S(1)}, u32[]{:S(2)}, u32[]{:S(2)}) collective-permute-start(bf16[256,1536]{1,0:T(8,128)(2,1)S(1)} %pad_maximum_fusion.1), channel_id=1, source_target_pairs={{0,80},{16,96},{32,112},{48,0},{64,16},{80,32},{96,48},{112,64},{1... | collective-permute-start | bytes 2359304 | tf_op jit(solution)/shard_map/ppermute | solution.py:34
  260.8 42.9 %collective-permute-start.15 = (bf16[256,1536]{1,0:T(8,128)(2,1)S(1)}, bf16[256,1536]{1,0:T(8,128)(2,1)S(1)}, u32[]{:S(2)}, u32[]{:S(2)}) collective-permute-start(bf16[256,1536]{1,0:T(8,128)(2,1)S(1)} %pad_maximum_fusion.1), channel_id=1, source_target_pairs={{0,96},{16,112},{32,0},{48,16},{64,32},{80,48},{96,64},{112,80},{1... | collective-permute-start | bytes 2359304 | tf_op jit(solution)/shard_map/ppermute | solution.py:34
  275.3 55.9 %collective-permute-start.16 = (bf16[256,1536]{1,0:T(8,128)(2,1)S(1)}, bf16[256,1536]{1,0:T(8,128)(2,1)S(1)}, u32[]{:S(2)}, u32[]{:S(2)}) collective-permute-start(bf16[256,1536]{1,0:T(8,128)(2,1)S(1)} %pad_maximum_fusion.1), channel_id=1, source_target_pairs={{0,112},{16,0},{32,16},{48,32},{64,48},{80,64},{96,80},{112,96},{1... | collective-permute-start | bytes 2359304 | tf_op jit(solution)/shard_map/ppermute | solution.py:34
  365.3 92.6 %copy-start.4 = (bf16[96,2048]{1,0:T(8,128)(2,1)S(1)}, bf16[96,2048]{1,0:T(8,128)(2,1)}, u32[]{:S(2)}) copy-start(bf16[96,2048]{1,0:T(8,128)(2,1)} %reduce-scatter.3.cloned.1.call-done) | copy-start | bytes 1179652
  (3 other events, 8.6 us)
Sparse Core Ops, SparseCore 0:
  11.1 74.9 all-gather.2
  134.4 85.6 reduce-scatter.2
  223.5 84.8 all-gather.4
  365.4 92.4 reduce-scatter.4

commit v3 on v2

v3 whole, which is shorter than its diff:
```python
import jax
import jax.numpy as jnp
from jax import lax
from jax.sharding import Mesh
from jax.sharding import PartitionSpec as P

QH = 16
KVH = 8
HD = 128
PAGE = 128
MAXLEN = 512


rope_base = 1000000.0
norm_eps = 1e-06


def swap_cores(value):
    return lax.ppermute(value, "core", [(0, 1), (1, 0)])


def from_behind(block, axis, distance):
    devices = range(lax.axis_size(axis))
    route = [(i - distance, i) for i in devices if i - distance in devices]
    return lax.ppermute(block, axis, route)


def gather_group(block):
    count = lax.axis_size("group")
    pieces = [block]
    for shift in range(1, count):
        route = [(source, (source + shift) % count) for source in range(count)]
        pieces.append(lax.ppermute(block, "group", route))
    stacked = jnp.stack(pieces)
    order = (lax.axis_index("group") - jnp.arange(count)) % count
    return jnp.take(stacked, order, axis=0).reshape(count * block.shape[0], block.shape[1])


def rms_scale(values, gain):
    square = jnp.mean(values * values, axis=-1, keepdims=True)
    return (values * lax.rsqrt(square + norm_eps) * gain).astype(jnp.bfloat16)


def rotate(values, places):
    half_dim = values.shape[-1] // 2
    frequency = rope_base ** (-(jnp.arange(half_dim, dtype=jnp.float32) * 2.0 / values.shape[-1]))
    angle = places.astype(jnp.float32)[:, None] * frequency[None, :]
    cosine = jnp.cos(angle)[:, None, :]
    sine = jnp.sin(angle)[:, None, :]
    widened = values.astype(jnp.float32)
    first = widened[..., :half_dim]
    second = widened[..., half_dim:]
    return jnp.concatenate(
        [first * cosine - second * sine, second * cosine + first * sine], axis=-1
    ).astype(jnp.bfloat16)


def by_core(own_part, other_part):
    first = lax.axis_index("core") == 0
    return jnp.where(first, own_part, other_part), jnp.where(first, other_part, own_part)


def dot(acts, weight):
    return jnp.dot(acts, weight, preferred_element_type=jnp.float32)


def dot_t(acts, weight_t):
    return lax.dot_general(
        acts, weight_t, (((1,), (1,)), ((), ())), preferred_element_type=jnp.float32
    )


def core_rows(values, chips, rows_dev):
    blocks = values.reshape(chips, 2, rows_dev, *values.shape[1:])
    own = lax.dynamic_index_in_dim(blocks, lax.axis_index("core"), axis=1, keepdims=False)
    return own.reshape(chips * rows_dev, *values.shape[1:])


def body(
    hidden,
    request_of,
    positions,
    page_table,
    attn_gain,
    mlp_gain,
    wq,
    wk,
    wv,
    wo,
    w_gate,
    w_up,
    w_down,
):
    chips = lax.axis_size("chip")
    rows_dev = hidden.shape[0]
    tok_group = request_of.shape[0]
    bf = jnp.bfloat16
    residual = hidden.astype(jnp.float32)
    normed = lax.all_gather(rms_scale(residual, attn_gain), "chip", axis=0, tiled=True)
    q_cols = wq.shape[1]
    kv_half = wk.shape[1]
    own_attn = jnp.concatenate([wq.astype(bf), wk.astype(bf), wv.astype(bf), wo.astype(bf).T], axis=1)
    own_attn = gather_group(own_attn)
    other_attn = swap_cores(own_attn)
    query_w = jnp.concatenate([own_attn[:, :q_cols], other_attn[:, :q_cols]], axis=1)
    out_w_t = jnp.concatenate(
        [own_attn[:, q_cols + 2 * kv_half :], other_attn[:, q_cols + 2 * kv_half :]], axis=1
    )
    key_lo, key_hi = by_core(own_attn[:, q_cols : q_cols + kv_half], other_attn[:, q_cols : q_cols + kv_half])
    value_lo, value_hi = by_core(
        own_attn[:, q_cols + kv_half : q_cols + 2 * kv_half],
        other_attn[:, q_cols + kv_half : q_cols + 2 * kv_half],
    )
    key_w = jnp.concatenate([key_lo, key_hi], axis=1)
    value_w = jnp.concatenate([value_lo, value_hi], axis=1)
    ff_cols = w_gate.shape[1]
    own_mlp = jnp.concatenate([w_gate.astype(bf), w_up.astype(bf), w_down.astype(bf).T], axis=1)
    own_mlp = gather_group(own_mlp)
    other_mlp = swap_cores(own_mlp)
    half_pos = core_rows(positions, chips, rows_dev)
    half_req = core_rows(request_of, chips, rows_dev)
    heads = 2 * q_cols // HD
    queries = rotate(dot(normed, query_w).astype(bf).reshape(-1, heads, HD), half_pos)
    keys_half = rotate(dot(normed, key_w).astype(bf).reshape(-1, 1, HD), half_pos)
    values_half = dot(normed, value_w).astype(bf).reshape(-1, 1, HD)
    kv_own = jnp.stack([keys_half[:, 0], values_half[:, 0]], axis=1)
    kv_other = swap_cores(kv_own)
    kv_lo, kv_hi = by_core(kv_own, kv_other)
    kv_rows = jnp.stack(
        [kv_lo.reshape(chips, rows_dev, 2, HD), kv_hi.reshape(chips, rows_dev, 2, HD)], axis=1
    ).reshape(tok_group, 2, HD)
    earlier_rows = min(MAXLEN, tok_group)
    earlier = from_behind(kv_rows[tok_group - earlier_rows :], "group", 1)
    all_rows = jnp.concatenate([earlier, kv_rows], axis=0)
    all_keys = all_rows[:, 0]
    all_values = all_rows[:, 1]
    first_request = request_of[0]
    first_position = positions[0]
    same_local = (half_req[:, None] == request_of[None, :]) & (
        positions[None, :] <= half_pos[:, None]
    )
    same_earlier = (half_req[:, None] == first_request) & (
        jnp.arange(earlier_rows)[None, :] >= earlier_rows - first_position
    )
    visible = jnp.concatenate([same_earlier, same_local], axis=1)
    scores = jnp.einsum(
        "qhd,kd->hqk", queries, all_keys, preferred_element_type=jnp.float32
    ) * HD ** (-0.5)
    scores = jnp.where(visible[None], scores, -1e30)
    row_peak = jnp.max(scores, axis=-1, keepdims=True)
    probs = jnp.where(visible[None], jnp.exp(scores - row_peak), 0.0)
    total = jnp.sum(probs, axis=-1, keepdims=True)
    mixed_heads = jnp.einsum(
        "hqk,kd->qhd", probs.astype(bf), all_values, preferred_element_type=jnp.float32
    ) / jnp.transpose(total, (1, 0, 2))
    attended = mixed_heads.astype(bf).reshape(-1, heads * HD)
    attn_part = dot_t(attended, out_w_t)
    attn_sum = lax.psum_scatter(attn_part.astype(bf), "chip", scatter_dimension=0, tiled=True)
    mixed = residual + attn_sum.astype(jnp.float32)
    normed_mlp = lax.all_gather(rms_scale(mixed, mlp_gain), "chip", axis=0, tiled=True)
    gate_sum = jnp.concatenate(
        [dot(normed_mlp, own_mlp[:, :ff_cols]), dot(normed_mlp, other_mlp[:, :ff_cols])], axis=1
    )
    up_sum = jnp.concatenate(
        [
            dot(normed_mlp, own_mlp[:, ff_cols : 2 * ff_cols]),
            dot(normed_mlp, other_mlp[:, ff_cols : 2 * ff_cols]),
        ],
        axis=1,
    )
    activation = (jax.nn.silu(gate_sum) * up_sum).astype(bf)
    down_w_t = jnp.concatenate([own_mlp[:, 2 * ff_cols :], other_mlp[:, 2 * ff_cols :]], axis=1)
    down_part = dot_t(activation, down_w_t)
    summed = lax.psum_scatter(down_part.astype(bf), "chip", scatter_dimension=0, tiled=True)
    layer_out = (mixed + summed.astype(jnp.float32)).astype(bf)
    pages = page_table.shape[1]
    changed = jnp.concatenate(
        [jnp.ones((1,), jnp.int32), (request_of[1:] != request_of[:-1]).astype(jnp.int32)]
    )
    opens = jnp.maximum(changed, (positions % PAGE == 0).astype(jnp.int32))
    logical = jnp.cumsum(opens) - 1
    chosen = jnp.sum(
        jnp.where(logical[:, None] == jnp.arange(pages)[None, :], page_table, 0), axis=1
    )
    target = chosen * PAGE + positions % PAGE
    own_slice = lax.dynamic_index_in_dim(kv_rows, lax.axis_index("core"), axis=1, keepdims=False)
    width = own_slice.shape[1]
    cache = jnp.zeros((pages * PAGE, width), jnp.bfloat16).at[target].set(own_slice)
    return (layer_out, cache.reshape(pages, PAGE, width))


def solution(mesh):
    groups, tensors = mesh.devices.shape
    split = Mesh(mesh.devices.reshape(groups, tensors // 2, 2), ("group", "chip", "core"))
    tensor = ("chip", "core")
    placed = (
        P(("group",) + tensor, None),
        P("group"),
        P("group"),
        P("group", None),
        P(),
        P(),
        P("group", tensor),
        P("group", tensor),
        P("group", tensor),
        P(tensor, "group"),
        P("group", tensor),
        P("group", tensor),
        P(tensor, "group"),
    )
    return jax.shard_map(
        body,
        mesh=split,
        in_specs=placed,
        out_specs=(P(("group",) + tensor, None), P("group", None, tensor)),
        check_vma=False,
    )
```

time: 468 us -> 443 us (0.947)
  the two profiles are of different devices: /device:TPU:2 before, /device:TPU:0 now
where the time goes in v3:
time: 443 us; the launch traced here: 434 us
  waiting for transfers between devices  255 us (58%)
  starting transfers between devices  47.3 us (11%)
  matrix products  43 us (10%)
  local copies, waits for them, and re-layouts  41.1 us (9%)
  other arithmetic  33.1 us (7%)
  between operations  15.3 us (3%)
    ppermute x14, waiting for transfers between devices, gather_group(): pieces.append(lax.ppermute(block, 'group', route))  89.1 us
    reduce_scatter x1, waiting for transfers between devices, body(): lax.psum_scatter(down_part.astype(bf), 'chip', scatter_dimension=0, tiled...  70.2 us
    all_gather x1, waiting for transfers between devices, body(): lax.all_gather(rms_scale(mixed, mlp_gain), 'chip', axis=0, tiled=True)  51.1 us
    ppermute x14, starting transfers between devices, gather_group(): pieces.append(lax.ppermute(block, 'group', route))  43.2 us
    all_gather x1, waiting for transfers between devices, body(): lax.all_gather(rms_scale(residual, attn_gain), 'chip', axis=0, tiled=True)  36.1 us
    dot_general x7, matrix products, dot(): return jnp.dot(acts, weight, preferred_element_type=jnp.float32)  20.9 us
    unnamed x54, local copies, waits for them, and re-layouts  10.4 us
    sub x1, matrix products, body(): probs = jnp.where(visible[None], jnp.exp(scores - row_peak), 0.0)  10.4 us
  transfers between devices with their start and end apart: 22, of which 12 were waited for; matrix products, arithmetic and copies ran while one was open for 14% of the time, Pallas kernels for 0%

profile of v3, /device:TPU:0, one launch (start us, length us, event | category | flops | bytes accessed | tf_op | source)
XLA Modules:
  0.0 434.4 jit_solution(3823843432435629774)
XLA Ops:
  13.3 3.6 collective-permute-start.1
  29.4 2.5 multiply_cosine_fusion
  35.6 6.9 %collective-permute-done.5 = bf16[256,384]{1,0:T(8,128)(2,1)S(1)} collective-permute-done((bf16[256,384]{1,0:T(8,128)(2,1)S(1)}, bf16[256,384]{1,0:T(8,128)(2,1)S(1)}, u32[]{:S(2)}, u32[]{:S(2)}) %collective-permute-start.5) | collective-permute-done | bytes 196640 | tf_op jit(solution)/shard_map/ppermute | solution.py:33
  42.6 2.1 collective-permute-done.6
  51.8 36.1 %all-gather.3.cloned.1.call-done = bf16[768,2048]{1,0:T(8,128)(2,1)} async-done(((bf16[96,2048]{1,0:T(8,128)(2,1)}), bf16[768,2048]{1,0:T(8,128)(2,1)}) %all-gather.3.cloned.1.call-update) | async-done | bytes 3145744 | tf_op jit(solution)/shard_map/all_gather | solution.py:99
  87.9 3.3 fusion.37
  103.8 3.5 collective-permute-start.9
  107.3 2.2 subtract_convert_fusion
  109.5 4.0 collective-permute-done.9
  114.2 10.4 %fusion.98 = (f32[2,768]{1,0:T(2,128)S(1)}, bf16[2,768,2048]{1,2,0:T(8,128)(2,1)}) fusion(pred[768,2048]{0,1:T(8,128)(4,1)} %pad_add_fusion, bf16[1536,2,128]{2,0,1:T(8,128)(2,1)S(1)} %bitcast.118, bf16[512,2,128]{2,0,1:T(8,128)(2,1)} %copy-done.17, bf16[768,2,64]{2,0,1:T(8,128)(2,1)} %get-tuple-element.9, bf16[768,2,64]{2,0,1:T(8,128)(2,1)} %get-tuple-element.8), kind=kOutput, calls=%fused_computation.166 | convolution fusion | flops 826017792 | bytes 9312256 | tf_op jit(solution)/shard_map/sub | solution.py:151
  124.6 3.8 fusion.33
  128.4 2.7 convolution_convert_fusion
  132.6 2.6 collective-permute-start.10
  135.1 2.9 collective-permute-start.11
  142.4 29.2 %collective-permute-done.10 = bf16[256,1536]{1,0:T(8,128)(2,1)S(1)} collective-permute-done((bf16[256,1536]{1,0:T(8,128)(2,1)S(1)}, bf16[256,1536]{1,0:T(8,128)(2,1)S(1)}, u32[]{:S(2)}, u32[]{:S(2)}) %collective-permute-start.10) | collective-permute-done | bytes 786464 | tf_op jit(solution)/shard_map/ppermute | solution.py:33
  172.6 7.2 %collective-permute-done.11 = bf16[256,1536]{1,0:T(8,128)(2,1)S(1)} collective-permute-done((bf16[256,1536]{1,0:T(8,128)(2,1)S(1)}, bf16[256,1536]{1,0:T(8,128)(2,1)S(1)}, u32[]{:S(2)}, u32[]{:S(2)}) %collective-permute-start.11) | collective-permute-done | bytes 786464 | tf_op jit(solution)/shard_map/ppermute | solution.py:33
  179.8 21.4 %collective-permute-start.16 = (bf16[256,1536]{1,0:T(8,128)(2,1)S(1)}, bf16[256,1536]{1,0:T(8,128)(2,1)S(1)}, u32[]{:S(2)}, u32[]{:S(2)}) collective-permute-start(bf16[256,1536]{1,0:T(8,128)(2,1)S(1)} %pad_maximum_fusion.2), channel_id=1, source_target_pairs={{0,112},{16,0},{32,16},{48,32},{64,48},{80,64},{96,80},{112,96},{1... | collective-permute-start | bytes 2359304 | tf_op jit(solution)/shard_map/ppermute | solution.py:33
  205.4 10.9 %collective-permute-done.15 = bf16[256,1536]{1,0:T(8,128)(2,1)S(1)} collective-permute-done((bf16[256,1536]{1,0:T(8,128)(2,1)S(1)}, bf16[256,1536]{1,0:T(8,128)(2,1)S(1)}, u32[]{:S(2)}, u32[]{:S(2)}) %collective-permute-start.15) | collective-permute-done | bytes 786464 | tf_op jit(solution)/shard_map/ppermute | solution.py:33
  217.3 32.3 %collective-permute-done.16 = bf16[256,1536]{1,0:T(8,128)(2,1)S(1)} collective-permute-done((bf16[256,1536]{1,0:T(8,128)(2,1)S(1)}, bf16[256,1536]{1,0:T(8,128)(2,1)S(1)}, u32[]{:S(2)}, u32[]{:S(2)}) %collective-permute-start.16) | collective-permute-done | bytes 786464 | tf_op jit(solution)/shard_map/ppermute | solution.py:33
  250.5 6.3 %gather_fusion.1 = bf16[8,256,1536]{2,1,0:T(8,128)(2,1)} fusion(bf16[8,256,1536]{2,1,0:T(8,128)(2,1)} %bitcast_dynamic-update-slice_fusion, s32[1024]{0:T(1024)S(1)} %pad_clamp_fusion), kind=kCustom, calls=%fused_computation.1 | custom fusion | bytes 12582944 | tf_op jit(solution)/shard_map/jit(_take)/gather | solution.py:36
  256.8 6.1 %bitcast_select_fusion.4 = bf16[2048,1536]{1,0:T(8,128)(2,1)} fusion(bf16[8,256,1536]{2,1,0:T(8,128)(2,1)} %gather_fusion.1, pred[2048]{0:T(1024)(128)(4,1)S(1)} %broadcast_in_dim.86), kind=kLoop, calls=%fused_computation.7 | loop fusion | flops 3145728 | bytes 12584960 | tf_op jit(solution)/shard_map/jit(_take)/select_n | solution.py:36
  266.4 3.1 slice.132
  269.5 4.0 collective-permute-done.17
  273.5 3.1 slice.133
  276.6 51.1 %all-gather.5.cloned.1.call-done = bf16[768,2048]{1,0:T(8,128)(2,1)} async-done(((bf16[96,2048]{1,0:T(8,128)(2,1)}), bf16[768,2048]{1,0:T(8,128)(2,1)}) %all-gather.5.cloned.1.call-update) | async-done | bytes 3145744 | tf_op jit(solution)/shard_map/all_gather | solution.py:160
  327.7 4.5 %fusion.21 = f32[768,512]{0,1:T(8,128)S(1)} fusion(bf16[768,2048]{1,0:T(8,128)(2,1)} %all-gather.5.cloned.1.call-done, bf16[2048,1536]{1,0:T(8,128)(2,1)} %bitcast_select_fusion.4), kind=kOutput, calls=%fused_computation.30 | convolution fusion | flops 1610612736 | bytes 6815744 | tf_op jit(solution)/shard_map/dot_general | solution.py:64
  332.3 3.5 fusion.19
  335.8 3.5 fusion.17
  339.4 3.7 fusion.15
  343.1 5.2 %fusion.11 = bf16[768,2048]{1,0:T(8,128)(2,1)} fusion(bf16[2048,512]{1,0:T(8,128)(2,1)S(1)} %copy-done.4, bf16[2048,512]{1,0:T(8,128)(2,1)S(1)} %copy-done.3, f32[768,512]{0,1:T(8,128)S(1)} %fusion.15, f32[768,512]{0,1:T(8,128)S(1)} %fusion.17, f32[768,512]{0,1:T(8,128)S(1)} %fusion.19, f32[768,512]{0,1:T(8,128)S(1)} %fusion.21), kind=kOutput, calls=%fused_computation.19 | convolution fusion | flops 3237478400 | bytes 13631488 | tf_op jit(solution)/shard_map/dot_general | solution.py:68
  349.2 6.1 %scatter_custom_fusion = bf16[8192,128]{1,0:T(8,128)(2,1)} fusion(s32[1536]{0:T(1024)S(1)} %compare_select_fusion, bf16[]{:T(256)} %constant.120.clone.1, bf16[1536,2,128]{2,0,1:T(8,128)(2,1)S(1)} %bitcast.120, s32[]{:T(128)} %constant.103.clone.1, s32[]{:T(128)S(6)} %select_n.118), kind=kCustom, calls=%fused_computation.55 | custom fusion | bytes 2490378 | tf_op jit(solution)/shard_map/scatter | solution.py:188
  355.4 70.2 %reduce-scatter.5.cloned.1.call-done = bf16[96,2048]{1,0:T(8,128)(2,1)} async-done(((bf16[768,2048]{1,0:T(8,128)(2,1)}), bf16[96,2048]{1,0:T(8,128)(2,1)}) %reduce-scatter.5.cloned.1.call-update) | async-done | bytes 393232 | tf_op jit(solution)/shard_map/reduce_scatter | solution.py:174
  (149 shorter events, 61.0 us)
Async XLA Ops:
  7.2 80.8 %all-gather.3.cloned.1.call-start = ((), (), s32[]{:S(2)}) async-start(), calls=%async_computation.2 | async-start | bytes 3538944 | tf_op jit(solution)/shard_map/all_gather | solution.py:99
  11.2 21.4 %collective-permute-start = (bf16[256,384]{1,0:T(8,128)(2,1)S(1)}, bf16[256,384]{1,0:T(8,128)(2,1)S(1)}, u32[]{:S(2)}, u32[]{:S(2)}) collective-permute-start(bf16[256,384]{1,0:T(8,128)(2,1)S(1)} %get-tuple-element.3), channel_id=1, source_target_pairs={{0,16},{16,32},{32,48},{48,64},{64,80},{80,96},{96,112},{112,0},{1... | collective-permute-start | bytes 589832 | tf_op jit(solution)/shard_map/ppermute | solution.py:33
  13.3 20.3 %collective-permute-start.1 = (bf16[256,384]{1,0:T(8,128)(2,1)S(1)}, bf16[256,384]{1,0:T(8,128)(2,1)S(1)}, u32[]{:S(2)}, u32[]{:S(2)}) collective-permute-start(bf16[256,384]{1,0:T(8,128)(2,1)S(1)} %get-tuple-element.3), channel_id=1, source_target_pairs={{0,32},{16,48},{32,64},{48,80},{64,96},{80,112},{96,0},{112,16},{1... | collective-permute-start | bytes 589832 | tf_op jit(solution)/shard_map/ppermute | solution.py:33
  16.9 18.6 %collective-permute-start.2 = (bf16[256,384]{1,0:T(8,128)(2,1)S(1)}, bf16[256,384]{1,0:T(8,128)(2,1)S(1)}, u32[]{:S(2)}, u32[]{:S(2)}) collective-permute-start(bf16[256,384]{1,0:T(8,128)(2,1)S(1)} %get-tuple-element.3), channel_id=1, source_target_pairs={{0,48},{16,64},{32,80},{48,96},{64,112},{80,0},{96,16},{112,32},{1... | collective-permute-start | bytes 589832 | tf_op jit(solution)/shard_map/ppermute | solution.py:33
  18.8 16.8 %collective-permute-start.3 = (bf16[256,384]{1,0:T(8,128)(2,1)S(1)}, bf16[256,384]{1,0:T(8,128)(2,1)S(1)}, u32[]{:S(2)}, u32[]{:S(2)}) collective-permute-start(bf16[256,384]{1,0:T(8,128)(2,1)S(1)} %get-tuple-element.3), channel_id=1, source_target_pairs={{0,64},{16,80},{32,96},{48,112},{64,0},{80,16},{96,32},{112,48},{1... | collective-permute-start | bytes 589832 | tf_op jit(solution)/shard_map/ppermute | solution.py:33
  19.3 16.3 %collective-permute-start.4 = (bf16[256,384]{1,0:T(8,128)(2,1)S(1)}, bf16[256,384]{1,0:T(8,128)(2,1)S(1)}, u32[]{:S(2)}, u32[]{:S(2)}) collective-permute-start(bf16[256,384]{1,0:T(8,128)(2,1)S(1)} %get-tuple-element.3), channel_id=1, source_target_pairs={{0,80},{16,96},{32,112},{48,0},{64,16},{80,32},{96,48},{112,64},{1... | collective-permute-start | bytes 589832 | tf_op jit(solution)/shard_map/ppermute | solution.py:33
  24.4 238.6 %reduce-scatter.3.cloned.1.call-start = ((), (), s32[]{:S(2)}) async-start(), calls=%async_computation.3 | async-start | bytes 3538944 | tf_op jit(solution)/shard_map/reduce_scatter | solution.py:158
  32.6 10.0 %collective-permute-start.5 = (bf16[256,384]{1,0:T(8,128)(2,1)S(1)}, bf16[256,384]{1,0:T(8,128)(2,1)S(1)}, u32[]{:S(2)}, u32[]{:S(2)}) collective-permute-start(bf16[256,384]{1,0:T(8,128)(2,1)S(1)} %get-tuple-element.3), channel_id=1, source_target_pairs={{0,96},{16,112},{32,0},{48,16},{64,32},{80,48},{96,64},{112,80},{1... | collective-permute-start | bytes 589832 | tf_op jit(solution)/shard_map/ppermute | solution.py:33
  33.6 11.1 %collective-permute-start.6 = (bf16[256,384]{1,0:T(8,128)(2,1)S(1)}, bf16[256,384]{1,0:T(8,128)(2,1)S(1)}, u32[]{:S(2)}, u32[]{:S(2)}) collective-permute-start(bf16[256,384]{1,0:T(8,128)(2,1)S(1)} %get-tuple-element.3), channel_id=1, source_target_pairs={{0,112},{16,0},{32,16},{48,32},{64,48},{80,64},{96,80},{112,96},{1... | collective-permute-start | bytes 589832 | tf_op jit(solution)/shard_map/ppermute | solution.py:33
  46.3 4.3 collective-permute-start.7
  87.9 4.1 copy-start
  91.2 3.1 copy-start.10
  92.0 3.4 copy-start.5
  94.1 3.7 collective-permute-start.8
  103.8 9.7 %collective-permute-start.9 = (bf16[512,2,128]{2,0,1:T(8,128)(2,1)S(1)}, bf16[512,2,128]{2,0,1:T(8,128)(2,1)S(1)}, u32[]{:S(2)}, u32[]{:S(2)}) collective-permute-start(bf16[512,2,128]{2,0,1:T(8,128)(2,1)S(1)} %slice.119), channel_id=1, source_target_pairs={{0,16},{16,32},{32,48},{48,64},{64,80},{80,96},{96,112},{1,17},{17... | collective-permute-start | bytes 786440 | tf_op jit(solution)/shard_map/ppermute | solution.py:25
  114.2 10.4 %copy-start.18 = (bf16[512,2,128]{2,0,1:T(8,128)(2,1)S(1)}, bf16[512,2,128]{2,0,1:T(8,128)(2,1)}, u32[]{:S(2)}) copy-start(bf16[512,2,128]{2,0,1:T(8,128)(2,1)} %copy-done.17) | copy-start | bytes 786436
  131.1 196.6 %all-gather.5.cloned.1.call-start = ((), (), s32[]{:S(2)}) async-start(), calls=%async_computation.4 | async-start | bytes 3538944 | tf_op jit(solution)/shard_map/all_gather | solution.py:160
  132.6 39.1 %collective-permute-start.10 = (bf16[256,1536]{1,0:T(8,128)(2,1)S(1)}, bf16[256,1536]{1,0:T(8,128)(2,1)S(1)}, u32[]{:S(2)}, u32[]{:S(2)}) collective-permute-start(bf16[256,1536]{1,0:T(8,128)(2,1)S(1)} %pad_maximum_fusion.2), channel_id=1, source_target_pairs={{0,16},{16,32},{32,48},{48,64},{64,80},{80,96},{96,112},{112,0},{1... | collective-permute-start | bytes 2359304 | tf_op jit(solution)/shard_map/ppermute | solution.py:33
  135.1 44.7 %collective-permute-start.11 = (bf16[256,1536]{1,0:T(8,128)(2,1)S(1)}, bf16[256,1536]{1,0:T(8,128)(2,1)S(1)}, u32[]{:S(2)}, u32[]{:S(2)}) collective-permute-start(bf16[256,1536]{1,0:T(8,128)(2,1)S(1)} %pad_maximum_fusion.2), channel_id=1, source_target_pairs={{0,32},{16,48},{32,64},{48,80},{64,96},{80,112},{96,0},{112,16},{1... | collective-permute-start | bytes 2359304 | tf_op jit(solution)/shard_map/ppermute | solution.py:33
  138.0 64.1 %collective-permute-start.12 = (bf16[256,1536]{1,0:T(8,128)(2,1)S(1)}, bf16[256,1536]{1,0:T(8,128)(2,1)S(1)}, u32[]{:S(2)}, u32[]{:S(2)}) collective-permute-start(bf16[256,1536]{1,0:T(8,128)(2,1)S(1)} %pad_maximum_fusion.2), channel_id=1, source_target_pairs={{0,48},{16,64},{32,80},{48,96},{64,112},{80,0},{96,16},{112,32},{1... | collective-permute-start | bytes 2359304 | tf_op jit(solution)/shard_map/ppermute | solution.py:33
  139.4 63.7 %collective-permute-start.13 = (bf16[256,1536]{1,0:T(8,128)(2,1)S(1)}, bf16[256,1536]{1,0:T(8,128)(2,1)S(1)}, u32[]{:S(2)}, u32[]{:S(2)}) collective-permute-start(bf16[256,1536]{1,0:T(8,128)(2,1)S(1)} %pad_maximum_fusion.2), channel_id=1, source_target_pairs={{0,64},{16,80},{32,96},{48,112},{64,0},{80,16},{96,32},{112,48},{1... | collective-permute-start | bytes 2359304 | tf_op jit(solution)/shard_map/ppermute | solution.py:33
  140.8 63.7 %collective-permute-start.14 = (bf16[256,1536]{1,0:T(8,128)(2,1)S(1)}, bf16[256,1536]{1,0:T(8,128)(2,1)S(1)}, u32[]{:S(2)}, u32[]{:S(2)}) collective-permute-start(bf16[256,1536]{1,0:T(8,128)(2,1)S(1)} %pad_maximum_fusion.2), channel_id=1, source_target_pairs={{0,80},{16,96},{32,112},{48,0},{64,16},{80,32},{96,48},{112,64},{1... | collective-permute-start | bytes 2359304 | tf_op jit(solution)/shard_map/ppermute | solution.py:33
  171.7 44.7 %collective-permute-start.15 = (bf16[256,1536]{1,0:T(8,128)(2,1)S(1)}, bf16[256,1536]{1,0:T(8,128)(2,1)S(1)}, u32[]{:S(2)}, u32[]{:S(2)}) collective-permute-start(bf16[256,1536]{1,0:T(8,128)(2,1)S(1)} %pad_maximum_fusion.2), channel_id=1, source_target_pairs={{0,96},{16,112},{32,0},{48,16},{64,32},{80,48},{96,64},{112,80},{1... | collective-permute-start | bytes 2359304 | tf_op jit(solution)/shard_map/ppermute | solution.py:33
  179.8 69.8 %collective-permute-start.16 = (bf16[256,1536]{1,0:T(8,128)(2,1)S(1)}, bf16[256,1536]{1,0:T(8,128)(2,1)S(1)}, u32[]{:S(2)}, u32[]{:S(2)}) collective-permute-start(bf16[256,1536]{1,0:T(8,128)(2,1)S(1)} %pad_maximum_fusion.2), channel_id=1, source_target_pairs={{0,112},{16,0},{32,16},{48,32},{64,48},{80,64},{96,80},{112,96},{1... | collective-permute-start | bytes 2359304 | tf_op jit(solution)/shard_map/ppermute | solution.py:33
  256.8 6.2 %copy-start.1 = (bf16[96,2048]{1,0:T(8,128)(2,1)S(1)}, bf16[96,2048]{1,0:T(8,128)(2,1)}, u32[]{:S(2)}) copy-start(bf16[96,2048]{1,0:T(8,128)(2,1)} %param.13) | copy-start | bytes 1179652
  256.8 7.4 %copy-start.14 = (f32[2048]{0:T(1024)S(1)}, f32[2048]{0:T(1024)}, u32[]{:S(2)}) copy-start(f32[2048]{0:T(1024)} %param.18) | copy-start | bytes 24580
  263.0 10.5 %collective-permute-start.17 = (bf16[2048,1536]{1,0:T(8,128)(2,1)}, bf16[2048,1536]{1,0:T(8,128)(2,1)}, u32[]{:S(2)}, u32[]{:S(2)}) collective-permute-start(bf16[2048,1536]{1,0:T(8,128)(2,1)} %bitcast_select_fusion.4), channel_id=1, source_target_pairs={{0,1},{1,0},{2,3},{3,2},{4,5},{5,4},{6,7},{7,6},{8,9},{9,8},{10,11... | collective-permute-start | bytes 18874376 | tf_op jit(solution)/shard_map/ppermute | solution.py:19
  266.2 159.4 %reduce-scatter.5.cloned.1.call-start = ((), (), s32[]{:S(2)}) async-start(), calls=%async_computation.5 | async-start | bytes 3538944 | tf_op jit(solution)/shard_map/reduce_scatter | solution.py:174
  327.7 4.5 %copy-start.16 = (bf16[768,2048]{1,0:T(8,128)(2,1)S(1)}, bf16[768,2048]{1,0:T(8,128)(2,1)}, u32[]{:S(2)}) copy-start(bf16[768,2048]{1,0:T(8,128)(2,1)} %all-gather.5.cloned.1.call-done) | copy-start | bytes 9437188
  339.4 3.7 copy-start.3
  339.4 3.7 copy-start.4
  348.3 77.3 %copy-start.2 = (bf16[96,2048]{1,0:T(8,128)(2,1)S(1)}, bf16[96,2048]{1,0:T(8,128)(2,1)}, u32[]{:S(2)}) copy-start(bf16[96,2048]{1,0:T(8,128)(2,1)} %reduce-scatter.3.cloned.1.call-done) | copy-start | bytes 1179652
  (9 other events, 14.4 us)
Sparse Core Ops, SparseCore 0:
  24.5 63.3 all-gather.2
  131.3 102.8 reduce-scatter.2
  266.3 61.3 all-gather.4
  348.4 77.0 reduce-scatter.4
